TPU v7x, 32 devices: a whole 2x2x4 slice. The times are simulated.
32 devices in a mesh: replica: 8 (over z, core), group: 4 (over y, x).
Axes of the slice: x: 2, y: 2, z: 4, core: 2. Of those that a mesh axis runs over, the one named last changes fastest.
Arguments:
- tokens: bfloat16 [4, 8192, 768], P('group', 'replica'), may hold values from -6 to 6
- cotangent: bfloat16 [4, 8192, 768], P('group', 'replica'), may hold values from -6 to 6
- lengths: int32 [4, 16], P('group'), may hold values from 256 to 768, as said below
- dealing: int32 [4, 16], P('group'), may hold values from 0 to 15, as said below
- offsets: int32 [4, 8, 2], P('group'), may hold values from 0 to 768, as said below
- attn_gain: float32 [768], P('group'), may hold values from 0.1 to 1.9
- qkv_weight: float32 [768, 2304], P('group'), may hold values from -0.21875 to 0.21875
- out_weight: float32 [768, 768], P('group'), may hold values from -0.875 to 0.875
- mlp_gain: float32 [768], P('group'), may hold values from 0.1 to 1.9
- in_weight: float32 [768, 2304], P('group'), may hold values from -0.21875 to 0.21875
- down_weight: float32 [1152, 768], P('group'), may hold values from -0.1875 to 0.1875
Outputs:
- output: bfloat16 [4, 8192, 768], P('group', 'replica')
- input_grad: bfloat16 [4, 8192, 768], P('group', 'replica')
- attn_gain_grad: float32 [768], P('group')
- qkv_grad: float32 [768, 2304], P('group')
- out_grad: float32 [768, 768], P('group')
- mlp_gain_grad: float32 [768], P('group')
- in_grad: float32 [768, 2304], P('group')
- down_grad: float32 [1152, 768], P('group')
Inputs may be any that keep to these rules, and one draw needn't show every extreme that they name: `lengths`: the 16 sequences of a column lie end to end over its 8192 tokens; the two sequences dealt to one replica index hold 1024 tokens together. `dealing`: for each column a permutation of its sequences: entry k is the given-order number of the sequence that is k-th in dealt order; replica index r takes dealt sequences 2 * r to 2 * r + 1. `offsets`: exclusive running sums of the lengths of each replica index's dealt sequences, in dealt order.
All inputs are finite; a program needn't handle non-finite values.
Results may differ from a plain program's by a relative error of at most 0.02.
Values may be sent and summed in bfloat16 or wider, within the bound.
No kernel may reach another device: no remote copies, remote signals or barrier semaphores. Data moves between devices by JAX's collectives and lax.ppermute only.
A program may use at most 256 MiB of HBM per device.

v0:
```python
import math

import jax
import jax.numpy as jnp
from jax import lax
from jax.sharding import PartitionSpec as P

HEADS = 12
HEAD_DIM = 64


epsilon = 1e-05
big_negative = -1e30
rope_base = 160000.0


def column_starts(lengths):
    return jnp.cumsum(lengths) - lengths


def dealt_map(lengths, dealing, offsets, replica_index, tok_rows):
    seq_count = lengths.shape[0]
    per_device = offsets.shape[1]
    starts = column_starts(lengths)
    slot_ids = jnp.arange(tok_rows, dtype=jnp.int32)
    own_starts = lax.dynamic_index_in_dim(offsets, replica_index, 0, keepdims=False)
    segment = jnp.sum((slot_ids[:, None] >= own_starts[None, 1:]).astype(jnp.int32), axis=1)
    choose = segment[:, None] == jnp.arange(per_device, dtype=jnp.int32)[None, :]
    begin_at = jnp.sum(jnp.where(choose, own_starts[None, :], 0), axis=1)
    positions = slot_ids - begin_at
    dealt = replica_index * per_device + segment
    seq_range = jnp.arange(seq_count, dtype=jnp.int32)
    dealt_hits = dealt[:, None] == seq_range[None, :]
    given = jnp.sum(jnp.where(dealt_hits, dealing[None, :], 0), axis=1)
    found_seq = given[:, None] == seq_range[None, :]
    first_at = jnp.sum(jnp.where(found_seq, starts[None, :], 0), axis=1)
    source = jnp.clip(first_at + positions, 0, tok_rows * offsets.shape[0] - 1)
    return (source, segment, positions)


def given_map(lengths, dealing, offsets, column_pos, tok_rows):
    seq_count = lengths.shape[0]
    per_device = offsets.shape[1]
    starts = column_starts(lengths)
    seq_range = jnp.arange(seq_count, dtype=jnp.int32)
    seq_id = jnp.sum((column_pos[:, None] >= starts[None, 1:]).astype(jnp.int32), axis=1)
    found_seq = seq_id[:, None] == seq_range[None, :]
    first_at = jnp.sum(jnp.where(found_seq, starts[None, :], 0), axis=1)
    positions = column_pos - first_at
    matches = dealing[None, :] == seq_id[:, None]
    dealt = jnp.sum(jnp.where(matches, seq_range[None, :], 0), axis=1)
    flat_starts = offsets.reshape(-1)
    dealt_hits = dealt[:, None] == seq_range[None, :]
    begin_at = jnp.sum(jnp.where(dealt_hits, flat_starts[None, :], 0), axis=1)
    target = dealt // per_device * tok_rows + begin_at + positions
    return jnp.clip(target, 0, tok_rows * offsets.shape[0] - 1)


def rotary(values, positions, head_count, head_dim):
    tok_rows = values.shape[0]
    half_dim = head_dim // 2
    frequency = jnp.exp(
        -(jnp.arange(half_dim, dtype=jnp.float32) * (2.0 / head_dim)) * math.log(rope_base)
    )
    angles = positions.astype(jnp.float32)[:, None] * frequency[None, :]
    cosine = jnp.cos(angles)[:, None, :]
    sine_part = jnp.sin(angles)[:, None, :]
    shaped = values.reshape(tok_rows, head_count, head_dim)
    lower_half = shaped[..., :half_dim]
    upper_half = shaped[..., half_dim:]
    turned = jnp.concatenate(
        [
            lower_half * cosine - upper_half * sine_part,
            upper_half * cosine + lower_half * sine_part,
        ],
        axis=-1,
    )
    return turned.reshape(tok_rows, head_count * head_dim)


def layer_norm(values, gain_vec):
    row_mean = jnp.mean(values, axis=-1, keepdims=True)
    centred = values - row_mean
    spread = jnp.mean(centred * centred, axis=-1, keepdims=True)
    return centred * lax.rsqrt(spread + epsilon) * gain_vec


def geglu(lifted):
    hidden_width = lifted.shape[1] // 2
    return jax.nn.gelu(lifted[:, :hidden_width], approximate=False) * lifted[:, hidden_width:]


def pick_rows(index_map, carry, piece):
    piece_rows = piece.shape[1]
    inside = (index_map >= 0) & (index_map < piece_rows)
    taken = jnp.take(piece[0], jnp.clip(index_map, 0, piece_rows - 1), axis=0)
    return jnp.where(inside[:, None], taken, carry)


def soft_block(queries, seg_query, key_heads, segment, score_scale):
    scores = (
        jnp.einsum("qhd,khd->hqk", queries, key_heads, preferred_element_type=jnp.float32)
        * score_scale
    )
    same_seq = seg_query[:, None] == segment[None, :]
    return jnp.where(same_seq[None], scores, big_negative)


def on_device(
    tokens,
    cotangent,
    lengths,
    dealing,
    offsets,
    attn_gain,
    qkv_weight,
    out_weight,
    mlp_gain,
    in_weight,
    down_weight,
):
    tok_rows = tokens.shape[1]
    model_width = tokens.shape[2]
    head_count = HEADS
    head_dim = HEAD_DIM
    score_scale = head_dim ** (-0.5)
    replica_index = lax.axis_index("replica")
    source, segment, positions = dealt_map(
        lengths[0], dealing[0], offsets[0], replica_index, tok_rows
    )
    target = given_map(
        lengths[0],
        dealing[0],
        offsets[0],
        replica_index * tok_rows + jnp.arange(tok_rows, dtype=jnp.int32),
        tok_rows,
    )
    masters = (
        attn_gain.astype(jnp.bfloat16),
        qkv_weight.astype(jnp.bfloat16),
        out_weight.astype(jnp.bfloat16),
        mlp_gain.astype(jnp.bfloat16),
        in_weight.astype(jnp.bfloat16),
        down_weight.astype(jnp.bfloat16),
    )
    weights = (
        lax.all_gather(masters[0], "group", axis=0, tiled=True),
        lax.all_gather(masters[1], "group", axis=0, tiled=True),
        lax.all_gather(masters[2], "group", axis=0, tiled=True),
        lax.all_gather(masters[3], "group", axis=0, tiled=True),
        lax.all_gather(masters[4], "group", axis=0, tiled=True),
        lax.all_gather(masters[5], "group", axis=0, tiled=True),
    )
    blank = jnp.zeros((tok_rows, model_width), jnp.bfloat16)
    dealt_x = pick_rows(source, blank, lax.all_gather(tokens, "replica", axis=1, tiled=True))
    gain_one, w_qkv, w_out, gain_two, w_in, w_down = weights
    gain_first = gain_one.astype(jnp.float32)
    gain_second = gain_two.astype(jnp.float32)
    rows_in = dealt_x.astype(jnp.float32)
    normed = layer_norm(rows_in, gain_first).astype(jnp.bfloat16)
    mixed_proj = jnp.dot(normed, w_qkv, preferred_element_type=jnp.float32)
    queries = (
        rotary(mixed_proj[:, :model_width], positions, head_count, head_dim)
        .astype(jnp.bfloat16)
        .reshape(tok_rows, head_count, head_dim)
    )
    key_heads = (
        rotary(mixed_proj[:, model_width : 2 * model_width], positions, head_count, head_dim)
        .astype(jnp.bfloat16)
        .reshape(tok_rows, head_count, head_dim)
    )
    value_heads = (
        mixed_proj[:, 2 * model_width :]
        .astype(jnp.bfloat16)
        .reshape(tok_rows, head_count, head_dim)
    )
    block_rows = min(512, tok_rows)
    block_count = tok_rows // block_rows
    attended_parts = []
    kept_tops = []
    kept_totals = []
    for number in range(block_count):
        lower_row = number * block_rows
        masked = soft_block(
            queries[lower_row : lower_row + block_rows],
            segment[lower_row : lower_row + block_rows],
            key_heads,
            segment,
            score_scale,
        )
        row_top = jnp.max(masked, axis=-1, keepdims=True)
        exponent = jnp.exp(masked - row_top)
        row_total = jnp.sum(exponent, axis=-1, keepdims=True)
        weights_soft = (exponent / row_total).astype(jnp.bfloat16)
        attended_block = jnp.einsum(
            "hqk,khd->qhd", weights_soft, value_heads, preferred_element_type=jnp.float32
        )
        attended_parts.append(attended_block.astype(jnp.bfloat16))
        kept_tops.append(row_top)
        kept_totals.append(row_total)
    attended = jnp.concatenate(attended_parts, axis=0).reshape(tok_rows, model_width)
    middle = rows_in + jnp.dot(attended, w_out, preferred_element_type=jnp.float32)
    normed_two = layer_norm(middle, gain_second).astype(jnp.bfloat16)
    lifted = jnp.dot(normed_two, w_in, preferred_element_type=jnp.float32)
    hidden = geglu(lifted).astype(jnp.bfloat16)
    output_dealt = (middle + jnp.dot(hidden, w_down, preferred_element_type=jnp.float32)).astype(
        jnp.bfloat16
    )
    output_given = pick_rows(
        target, blank, lax.all_gather(output_dealt[None], "replica", axis=1, tiled=True)
    )
    dealt_dy = pick_rows(source, blank, lax.all_gather(cotangent, "replica", axis=1, tiled=True))
    weights = (
        lax.all_gather(masters[0], "group", axis=0, tiled=True),
        lax.all_gather(masters[1], "group", axis=0, tiled=True),
        lax.all_gather(masters[2], "group", axis=0, tiled=True),
        lax.all_gather(masters[3], "group", axis=0, tiled=True),
        lax.all_gather(masters[4], "group", axis=0, tiled=True),
        lax.all_gather(masters[5], "group", axis=0, tiled=True),
    )
    gain_one, w_qkv, w_out, gain_two, w_in, w_down = weights
    grad_out = dealt_dy.astype(jnp.float32)
    down_partial = jnp.einsum("tf,td->fd", hidden, dealt_dy, preferred_element_type=jnp.float32)
    grad_hidden = jnp.einsum("td,fd->tf", dealt_dy, w_down, preferred_element_type=jnp.float32)
    _, geglu_back = jax.vjp(geglu, lifted)
    grad_lifted = geglu_back(grad_hidden)[0].astype(jnp.bfloat16)
    in_partial = jnp.einsum(
        "td,tf->df", normed_two, grad_lifted, preferred_element_type=jnp.float32
    )
    grad_normed_two = jnp.einsum("tf,df->td", grad_lifted, w_in, preferred_element_type=jnp.float32)
    _, norm_back_two = jax.vjp(layer_norm, middle, gain_second)
    grad_middle_part, gain_two_partial = norm_back_two(grad_normed_two)
    grad_middle = grad_out + grad_middle_part
    grad_branch = grad_middle.astype(jnp.bfloat16)
    out_partial = jnp.einsum("ti,to->io", attended, grad_branch, preferred_element_type=jnp.float32)
    grad_attended = (
        jnp.einsum("to,io->ti", grad_branch, w_out, preferred_element_type=jnp.float32)
        .astype(jnp.bfloat16)
        .reshape(tok_rows, head_count, head_dim)
    )
    grad_keys = jnp.zeros((tok_rows, head_count, head_dim), jnp.float32)
    grad_values = jnp.zeros((tok_rows, head_count, head_dim), jnp.float32)
    grad_query_parts = []
    for number in range(block_count):
        lower_row = number * block_rows
        query_block = queries[lower_row : lower_row + block_rows]
        masked = soft_block(
            query_block,
            segment[lower_row : lower_row + block_rows],
            key_heads,
            segment,
            score_scale,
        )
        weights_full = jnp.exp(masked - kept_tops[number]) / kept_totals[number]
        weights_soft = weights_full.astype(jnp.bfloat16)
        grad_block = grad_attended[lower_row : lower_row + block_rows]
        grad_probs = jnp.einsum(
            "qhd,khd->hqk", grad_block, value_heads, preferred_element_type=jnp.float32
        )
        inner = jnp.sum(weights_full * grad_probs, axis=-1, keepdims=True)
        grad_scores = (weights_full * (grad_probs - inner)).astype(jnp.bfloat16)
        grad_query_parts.append(
            jnp.einsum("hqk,khd->qhd", grad_scores, key_heads, preferred_element_type=jnp.float32)
            * score_scale
        )
        grad_keys = (
            grad_keys
            + jnp.einsum(
                "hqk,qhd->khd", grad_scores, query_block, preferred_element_type=jnp.float32
            )
            * score_scale
        )
        grad_values = grad_values + jnp.einsum(
            "hqk,qhd->khd", weights_soft, grad_block, preferred_element_type=jnp.float32
        )
    grad_queries = jnp.concatenate(grad_query_parts, axis=0).reshape(tok_rows, model_width)

    def turn_rows(values):
        return rotary(values, positions, head_count, head_dim)

    _, rope_back = jax.vjp(turn_rows, mixed_proj[:, :model_width])
    grad_mixed = jnp.concatenate(
        [
            rope_back(grad_queries)[0],
            rope_back(grad_keys.reshape(tok_rows, model_width))[0],
            grad_values.reshape(tok_rows, model_width),
        ],
        axis=1,
    ).astype(jnp.bfloat16)
    qkv_partial = jnp.einsum("td,te->de", normed, grad_mixed, preferred_element_type=jnp.float32)
    grad_normed = jnp.einsum("te,de->td", grad_mixed, w_qkv, preferred_element_type=jnp.float32)
    _, norm_back_one = jax.vjp(layer_norm, rows_in, gain_first)
    grad_rows_part, gain_one_partial = norm_back_one(grad_normed)
    grad_input = (grad_middle + grad_rows_part).astype(jnp.bfloat16)
    grad_given = pick_rows(
        target, blank, lax.all_gather(grad_input[None], "replica", axis=1, tiled=True)
    )
    partial_grads = (
        gain_one_partial,
        qkv_partial,
        out_partial,
        gain_two_partial,
        in_partial,
        down_partial,
    )
    shards = (
        lax.psum_scatter(
            partial_grads[0].astype(jnp.bfloat16), "group", scatter_dimension=0, tiled=True
        ).astype(jnp.float32),
        lax.psum_scatter(
            partial_grads[1].astype(jnp.bfloat16), "group", scatter_dimension=0, tiled=True
        ).astype(jnp.float32),
        lax.psum_scatter(
            partial_grads[2].astype(jnp.bfloat16), "group", scatter_dimension=0, tiled=True
        ).astype(jnp.float32),
        lax.psum_scatter(
            partial_grads[3].astype(jnp.bfloat16), "group", scatter_dimension=0, tiled=True
        ).astype(jnp.float32),
        lax.psum_scatter(
            partial_grads[4].astype(jnp.bfloat16), "group", scatter_dimension=0, tiled=True
        ).astype(jnp.float32),
        lax.psum_scatter(
            partial_grads[5].astype(jnp.bfloat16), "group", scatter_dimension=0, tiled=True
        ).astype(jnp.float32),
    )
    summed = (
        lax.psum(shards[0].astype(jnp.bfloat16), "replica").astype(jnp.float32),
        lax.psum(shards[1].astype(jnp.bfloat16), "replica").astype(jnp.float32),
        lax.psum(shards[2].astype(jnp.bfloat16), "replica").astype(jnp.float32),
        lax.psum(shards[3].astype(jnp.bfloat16), "replica").astype(jnp.float32),
        lax.psum(shards[4].astype(jnp.bfloat16), "replica").astype(jnp.float32),
        lax.psum(shards[5].astype(jnp.bfloat16), "replica").astype(jnp.float32),
    )
    return (
        output_given[None],
        grad_given[None],
        summed[0],
        summed[1],
        summed[2],
        summed[3],
        summed[4],
        summed[5],
    )


def solution(mesh):
    return jax.shard_map(
        on_device,
        mesh=mesh,
        in_specs=(
            P("group", "replica", None),
            P("group", "replica", None),
            P("group", None),
            P("group", None),
            P("group", None, None),
            P("group"),
            P("group", None),
            P("group", None),
            P("group"),
            P("group", None),
            P("group", None),
        ),
        out_specs=(
            P("group", "replica", None),
            P("group", "replica", None),
            P("group"),
            P("group", None),
            P("group", None),
            P("group"),
            P("group", None),
            P("group", None),
        ),
        check_vma=False,
    )
```

profile of v0, /device:TPU:0, one launch (start us, length us, event | category | flops | bytes accessed | tf_op | source)
XLA Modules:
  0.0 1018.6 jit_solution(18329896838933659207)
XLA Ops:
  8.0 2.6 convert_element_type.175
  21.5 11.4 %all-reduce.13 = (bf16[768]{0:T(1024)(128)(2,1)S(1)}, bf16[768]{0:T(1024)(128)(2,1)S(1)}) all-reduce(bf16[768]{0:T(1024)(128)(2,1)S(1)} %dynamic-update-slice, bf16[768]{0:T(1024)(128)(2,1)S(1)} %dynamic-update-slice.1), channel_id=1, replica_groups=mesh['replica'=8,'group'=4] {'group'}, use_global_device_ids=true, to_apply=%add.6 | all-reduce | flops 1536 | bytes 6144
  35.0 94.1 %all-gather.11.cloned.1.call-done = bf16[1,8192,768]{2,1,0:T(8,128)(2,1)} async-done(((bf16[1,1024,768]{2,1,0:T(8,128)(2,1)}), bf16[1,8192,768]{2,1,0:T(8,128)(2,1)}) %all-gather.11.cloned.1.call-update) | async-done | bytes 12582928 | tf_op jit(solution)/shard_map/all_gather | solution.py:155
  129.1 10.7 %gather_fusion = bf16[1024,768]{1,0:T(8,128)(2,1)S(1)} fusion(bf16[8192,768]{1,0:T(8,128)(2,1)} %bitcast.69, s32[1024]{0:T(1024)S(1)} %get-tuple-element.93), kind=kCustom, calls=%fused_computation.clone | custom fusion | bytes 3149824 | tf_op jit(solution)/shard_map/jit(_take)/gather | solution.py:96
  141.7 35.2 %all-gather.13.cloned.1.call-done = bf16[768,2304]{1,0:T(8,128)(2,1)} async-done(((bf16[192,2304]{1,0:T(8,128)(2,1)}), bf16[768,2304]{1,0:T(8,128)(2,1)}) %all-gather.13.cloned.1.call-update) | async-done | bytes 3538960 | tf_op jit(solution)/shard_map/all_gather | solution.py:148
  176.9 6.2 fusion.60
  183.3 3.2 fusion.104
  186.5 4.0 copy.71
  192.1 3.5 copy.70
  195.6 3.9 subtract_convert_fusion
  199.6 10.4 %fusion.62 = f32[12,512,1024]{2,1,0:T(8,128)} fusion(bf16[1024,12,32]{0,2,1:T(8,128)(2,1)S(1)} %get-tuple-element.82, bf16[1024,12,32]{0,2,1:T(8,128)(2,1)S(1)} %get-tuple-element.83, bf16[1024,12,32]{0,2,1:T(8,128)(2,1)S(1)} %get-tuple-element.75, bf16[1024,12,32]{0,2,1:T(8,128)(2,1)S(1)} %get-tuple-element.74), kind=kOutput, calls=%fused_computation.126 | convolution fusion | flops 810024960 | bytes 28311552 | tf_op jit(solution)/shard_map/qhd,khd->hqk/dot_general | solution.py:102
  210.0 14.6 %fusion.109 = (f32[12,512]{1,0:T(8,128)S(1)}, f32[12,512,1024]{2,1,0:T(8,128)}) fusion(pred[512,1024]{1,0:T(8,128)(4,1)} %get-tuple-element.88, bf16[1024,12,32]{0,2,1:T(8,128)(2,1)} %copy-done.17, bf16[1024,12,32]{0,2,1:T(8,128)(2,1)} %copy-done.15, bf16[1024,12,32]{0,2,1:T(8,128)(2,1)S(1)} %get-tuple-element.83, ...), kind=kOutput, calls=%fused_computation.205 | convolution fusion | flops 835191808 | bytes 28860416 | tf_op jit(solution)/shard_map/sub | solution.py:192
  224.6 33.6 %fusion.108 = (f32[12,512]{1,0:T(8,128)S(1)}, f32[12,512,1024]{2,1,0:T(8,128)}) fusion(f32[12,512,1024]{2,1,0:T(8,128)} %fusion.62, pred[512,1024]{1,0:T(8,128)(4,1)} %get-tuple-element.89), kind=kOutput, calls=%fused_computation.204 | output fusion | flops 37749760 | bytes 50880512 | tf_op jit(solution)/shard_map/sub | solution.py:192
  258.2 11.4 %fusion.52 = bf16[512,12,64]{0,2,1:T(8,128)(2,1)} fusion(bf16[1024,12,64]{0,2,1:T(8,128)(2,1)S(1)} %bitcast.72, f32[12,512,1024]{2,1,0:T(8,128)} %get-tuple-element.101, f32[12,512]{1,0:T(8,128)S(1)} %get-tuple-element.100), kind=kOutput, calls=%fused_computation.115 | convolution fusion | flops 818282496 | bytes 27549696 | tf_op jit(solution)/shard_map/hqk,khd->qhd/dot_general | solution.py:195
  269.6 11.6 %fusion.49 = bf16[512,12,64]{0,2,1:T(8,128)(2,1)} fusion(bf16[1024,12,64]{0,2,1:T(8,128)(2,1)S(1)} %bitcast.73, f32[12,512,1024]{2,1,0:T(8,128)} %get-tuple-element.99, f32[12,512]{1,0:T(8,128)S(1)} %get-tuple-element.98), kind=kOutput, calls=%fused_computation.114 | convolution fusion | flops 818282496 | bytes 27549696 | tf_op jit(solution)/shard_map/hqk,khd->qhd/dot_general | solution.py:195
  281.2 14.1 %all-gather.21.cloned.1.call-done = bf16[1,8192,768]{2,1,0:T(8,128)(2,1)} async-done(((bf16[1,1024,768]{2,1,0:T(8,128)(2,1)}), bf16[1,8192,768]{2,1,0:T(8,128)(2,1)}) %all-gather.21.cloned.1.call-update) | async-done | bytes 12582928 | tf_op jit(solution)/shard_map/all_gather | solution.py:212
  295.3 11.8 %gather_fusion.2 = bf16[1024,768]{1,0:T(8,128)(2,1)} fusion(bf16[8192,768]{1,0:T(8,128)(2,1)} %bitcast.68, s32[1024]{0:T(1024)S(1)} %get-tuple-element.93), kind=kCustom, calls=%fused_computation.2.clone | custom fusion | bytes 3149824 | tf_op jit(solution)/shard_map/jit(_take)/gather | solution.py:96
  307.0 1.7 copy.75
  308.8 3.3 pad_maximum_fusion.5
  312.0 10.8 %all-gather.15.cloned.1.call-done = bf16[768,768]{1,0:T(8,128)(2,1)} async-done(((bf16[192,768]{1,0:T(8,128)(2,1)}), bf16[768,768]{1,0:T(8,128)(2,1)}) %all-gather.15.cloned.1.call-update) | async-done | bytes 1179664 | tf_op jit(solution)/shard_map/all_gather | solution.py:149
  322.8 3.4 fusion.114
  328.2 44.0 %all-gather.17.cloned.1.call-done = bf16[768,2304]{1,0:T(8,128)(2,1)} async-done(((bf16[192,2304]{1,0:T(8,128)(2,1)}), bf16[768,2304]{1,0:T(8,128)(2,1)}) %all-gather.17.cloned.1.call-update) | async-done | bytes 3538960 | tf_op jit(solution)/shard_map/all_gather | solution.py:151
  372.2 10.6 %fusion.93 = f32[1024,2304]{1,0:T(8,128)} fusion(bf16[768,2304]{1,0:T(8,128)(2,1)} %all-gather.17.cloned.1.call-done, f32[1024,768]{0,1:T(8,128)} %copy-done.12, f32[768]{0:T(1024)S(1)} %convert_element_type.186, f32[1024]{0:T(1024)S(1)} %fusion.73, f32[1024]{0:T(1024)S(1)} %broadcast_multiply_fusion), kind=kOutput, calls=%fused_computation.196 | convolution fusion | flops 3627024384 | bytes 16133120 | tf_op jit(solution)/shard_map/dot_general | solution.py:204
  382.8 23.6 %all-gather.19.cloned.1.call-done = bf16[1152,768]{1,0:T(8,128)(2,1)} async-done(((bf16[288,768]{1,0:T(8,128)(2,1)}), bf16[1152,768]{1,0:T(8,128)(2,1)}) %all-gather.19.cloned.1.call-update) | async-done | bytes 1769488 | tf_op jit(solution)/shard_map/all_gather | solution.py:152
  406.4 14.5 %fusion.42 = (f32[1024,1152]{1,0:T(8,128)}, f32[1024,1152]{1,0:T(8,128)S(1)}, f32[1024,1152]{1,0:T(8,128)S(1)}) fusion(f32[1024,2304]{1,0:T(8,128)} %fusion.93, bf16[1152,768]{1,0:T(8,128)(2,1)} %all-gather.19.cloned.1.call-done, bf16[1024,768]{0,1:T(8,128)(2,1)S(1)} %copy.75, pred[1024]{0:T(1024)(128)(4,1)S(1)} %get-tuple-element.85, ...), kind=kOutput, calls=%fused_computation.111 | convolution fusion | flops 1890189312 | bytes 22218752 | tf_op jit(solution)/shard_map/td,fd->tf/dot_general | solution.py:224
  420.9 3.5 multiply_add_fusion
  424.4 9.6 multiply_reduce_fusion.2
  437.0 3.3 convolution_convert_fusion.2
  440.3 2.2 fusion.35
  443.6 2.5 convolution_convert_fusion.4
  446.1 2.8 convolution_convert_fusion.3
  449.1 1.8 copy-done.25
  450.8 19.3 %multiply_reduce_fusion.1 = (f32[12,512]{1,0:T(8,128)S(1)}, f32[12,512,1024]{2,1,0:T(8,128)}) fusion(f32[12,512,1024]{2,1,0:T(8,128)} %get-tuple-element.101, f32[12,512]{1,0:T(8,128)S(1)} %get-tuple-element.100, bf16[512,12,64]{0,2,1:T(8,128)(2,1)S(1)} %bitcast.82, bf16[1024,12,64]{0,2,1:T(8,128)(2,1)S(1)} %bitcast.74), kind=kOutput, calls=%fused_computation.9 | convolution fusion | flops 824174592 | bytes 52740096 | tf_op jit(solution)/shard_map/qhd,khd->hqk/dot_general | solution.py:257
  470.1 19.1 %multiply_reduce_fusion = (f32[12,512]{1,0:T(8,128)S(1)}, f32[12,512,1024]{2,1,0:T(8,128)}) fusion(f32[12,512,1024]{2,1,0:T(8,128)} %get-tuple-element.99, f32[12,512]{1,0:T(8,128)S(1)} %get-tuple-element.98, bf16[512,12,64]{0,2,1:T(8,128)(2,1)S(1)} %bitcast.84, bf16[1024,12,64]{0,2,1:T(8,128)(2,1)S(1)} %bitcast.75), kind=kOutput, calls=%fused_computation.7 | convolution fusion | flops 824174592 | bytes 52740096 | tf_op jit(solution)/shard_map/qhd,khd->hqk/dot_general | solution.py:257
  489.3 17.0 %multiply_convert_fusion.1 = bf16[12,512,1024]{2,1,0:T(8,128)(2,1)S(1)} fusion(f32[12,512,1024]{2,1,0:T(8,128)} %get-tuple-element.109, f32[12,512]{1,0:T(8,128)S(1)} %get-tuple-element.108, f32[12,512,1024]{2,1,0:T(8,128)} %get-tuple-element.101, f32[12,512]{1,0:T(8,128)S(1)} %get-tuple-element.100), kind=kLoop, calls=%fused_computation.8 | loop fusion | flops 25165824 | bytes 62963712 | tf_op jit(solution)/shard_map/convert_element_type | solution.py:261
  506.4 27.2 %multiply_convert_fusion = bf16[12,512,1024]{2,1,0:T(8,128)(2,1)} fusion(f32[12,512,1024]{2,1,0:T(8,128)} %get-tuple-element.107, f32[12,512]{1,0:T(8,128)S(1)} %get-tuple-element.106, f32[12,512,1024]{2,1,0:T(8,128)} %get-tuple-element.99, f32[12,512]{1,0:T(8,128)S(1)} %get-tuple-element.98), kind=kLoop, calls=%fused_computation.6 | loop fusion | flops 25165824 | bytes 62963712 | tf_op jit(solution)/shard_map/convert_element_type | solution.py:261
  533.6 2.3 fusion.97
  536.0 9.6 multiply_bitcast_fusion.2
  545.6 9.6 multiply_bitcast_fusion.1
  555.3 7.2 multiply_bitcast_fusion
  562.5 9.7 convolution_convert_fusion
  573.2 3.1 multiply_add_fusion.4
  577.7 10.7 %fusion.10 = f32[12,64,1024]{2,1,0:T(8,128)S(1)} fusion(bf16[512,12,64]{0,2,1:T(8,128)(2,1)S(1)} %bitcast.85, f32[12,512,1024]{2,1,0:T(8,128)} %get-tuple-element.99, f32[12,512]{1,0:T(8,128)S(1)} %get-tuple-element.98), kind=kOutput, calls=%fused_computation.26 | convolution fusion | flops 817889280 | bytes 29122560 | tf_op jit(solution)/shard_map/hqk,qhd->khd/dot_general | solution.py:273
  588.4 10.6 %add_convert_fusion.2 = bf16[12,64,1024]{2,1,0:T(8,128)(2,1)S(1)} fusion(f32[12,64,1024]{2,1,0:T(8,128)S(1)} %fusion.10, bf16[512,12,64]{0,2,1:T(8,128)(2,1)S(1)} %bitcast.83, f32[12,512,1024]{2,1,0:T(8,128)} %get-tuple-element.101, f32[12,512]{1,0:T(8,128)S(1)} %get-tuple-element.100), kind=kOutput, calls=%fused_computation.76 | convolution fusion | flops 819462144 | bytes 30695424 | tf_op jit(solution)/shard_map/hqk,qhd->khd/dot_general | solution.py:273
  600.3 8.7 convolution_convert_fusion.1
  609.1 10.5 %reduce-scatter.9.cloned.1.call-done = bf16[192,2304]{1,0:T(8,128)(2,1)} async-done(((bf16[768,2304]{1,0:T(8,128)(2,1)}), bf16[192,2304]{1,0:T(8,128)(2,1)}) %reduce-scatter.9.cloned.1.call-update) | async-done | bytes 884752 | tf_op jit(solution)/shard_map/reduce_scatter | solution.py:319
  619.6 50.1 %reduce-scatter.5.cloned.1.call-done = bf16[192,2304]{1,0:T(8,128)(2,1)} async-done(((bf16[768,2304]{1,0:T(8,128)(2,1)}), bf16[192,2304]{1,0:T(8,128)(2,1)}) %reduce-scatter.5.cloned.1.call-update) | async-done | bytes 884752 | tf_op jit(solution)/shard_map/reduce_scatter | solution.py:310
  669.8 6.6 add_convert_fusion.5
  676.4 7.2 fusion.34
  686.1 3.0 add_convert_fusion.1
  689.8 8.9 all-reduce.12
  698.9 14.6 %all-reduce.10 = (bf16[192]{0:T(256)(128)(2,1)S(1)}, bf16[192]{0:T(256)(128)(2,1)S(1)}) all-reduce(bf16[192]{0:T(256)(128)(2,1)S(1)} %dynamic-slice.4, bf16[192]{0:T(256)(128)(2,1)S(1)} %dynamic-slice.6), channel_id=1, replica_groups=mesh['replica'=8,'group'=4] {'replica'}, use_global_device_ids=true, to_apply=%region_24.26 | all-reduce | flops 384 | bytes 1536 | tf_op jit(solution)/shard_map/psum | solution.py:327
  714.6 25.9 %all-reduce.16.cloned.1.call-done = (bf16[192,2304]{1,0:T(8,128)(2,1)}, bf16[192,768]{1,0:T(8,128)(2,1)}, bf16[192,2304]{1,0:T(8,128)(2,1)}, bf16[288,768]{1,0:T(8,128)(2,1)}) async-done(((bf16[192,2304]{1,0:T(8,128)(2,1)}, bf16[192,768]{1,0:T(8,128)(2,1)}, bf16[192,2304]{1,0:T(8,128)(2,1)}, bf16[288,768]{1,0:T(8,128)(2,1)}), (bf16[192,2304]{1,0:T(8,128)(2,1)}, bf16[192,768]{1,0:T(8,128)(2,1)}, ...) | async-done | bytes 2506768 | tf_op jit(solution)/shard_map/psum | solution.py:328
  740.5 1.9 convert_element_type.204
  742.4 2.5 convert_element_type.202
  747.2 111.1 %all-gather.23.cloned.1.call-done = bf16[8192,768]{0,1:T(8,128)(2,1)} async-done(((bf16[1024,768]{0,1:T(8,128)(2,1)}), bf16[8192,768]{0,1:T(8,128)(2,1)}) %all-gather.23.cloned.1.call-update) | async-done | bytes 12582928 | tf_op jit(solution)/shard_map/all_gather | solution.py:210
  858.3 16.6 %copy.73 = bf16[8192,768]{1,0:T(8,128)(2,1)} copy(bf16[8192,768]{0,1:T(8,128)(2,1)} %all-gather.23.cloned.1.call-done) | data formatting | bytes 25165824 | tf_op jit(solution)/shard_map/all_gather | solution.py:210
  874.9 10.8 %gather_fusion.1 = bf16[1024,768]{1,0:T(8,128)(2,1)S(1)} fusion(bf16[8192,768]{1,0:T(8,128)(2,1)} %copy.73, s32[1024]{0:T(1024)S(1)} %fusion.75), kind=kCustom, calls=%fused_computation.1.clone | custom fusion | bytes 3149824 | tf_op jit(solution)/shard_map/jit(_take)/gather | solution.py:96
  886.5 88.9 %all-gather.25.cloned.1.call-done = bf16[8192,768]{0,1:T(8,128)(2,1)} async-done(((bf16[1024,768]{0,1:T(8,128)(2,1)}), bf16[8192,768]{0,1:T(8,128)(2,1)}) %all-gather.25.cloned.1.call-update) | async-done | bytes 12582928 | tf_op jit(solution)/shard_map/all_gather | solution.py:296
  975.4 16.7 %copy.76 = bf16[8192,768]{1,0:T(8,128)(2,1)} copy(bf16[8192,768]{0,1:T(8,128)(2,1)} %all-gather.25.cloned.1.call-done) | data formatting | bytes 25165824 | tf_op jit(solution)/shard_map/all_gather | solution.py:296
  992.1 11.8 %gather_fusion.3 = bf16[1024,768]{1,0:T(8,128)(2,1)} fusion(bf16[8192,768]{1,0:T(8,128)(2,1)} %copy.76, s32[1024]{0:T(1024)S(1)} %fusion.75), kind=kCustom, calls=%fused_computation.3.clone | custom fusion | bytes 3149824 | tf_op jit(solution)/shard_map/jit(_take)/gather | solution.py:96
  1003.8 1.7 copy.77
  1005.5 2.0 fusion.40
  1007.6 2.7 copy.79
  (229 shorter events, 34.9 us)
Async XLA Ops:
  7.2 4.3 copy-start.39
  7.2 121.9 %all-gather.11.cloned.1.call-start = ((), (), s32[]{:S(2)}) async-start(), calls=%async_computation.4 | async-start | bytes 14155776 | tf_op jit(solution)/shard_map/all_gather | solution.py:155
  7.9 4.4 copy-start.23
  7.9 169.0 %all-gather.13.cloned.1.call-start = ((), (), s32[]{:S(2)}) async-start(), calls=%async_computation.5 | async-start | bytes 4423680 | tf_op jit(solution)/shard_map/all_gather | solution.py:148
  10.6 284.7 %all-gather.21.cloned.1.call-start = ((), (), s32[]{:S(2)}) async-start(), calls=%async_computation.9 | async-start | bytes 14155776 | tf_op jit(solution)/shard_map/all_gather | solution.py:212
  11.3 3.0 copy-start.59
  11.4 5.1 copy-start.62
  11.4 6.3 copy-start.63
  11.4 8.3 copy-start.65
  11.4 8.3 copy-start.66
  11.4 8.3 copy-start.60
  11.4 311.4 %all-gather.15.cloned.1.call-start = ((), (), s32[]{:S(2)}) async-start(), calls=%async_computation.6 | async-start | bytes 1474560 | tf_op jit(solution)/shard_map/all_gather | solution.py:149
  12.2 360.0 %all-gather.17.cloned.1.call-start = ((), (), s32[]{:S(2)}) async-start(), calls=%async_computation.7 | async-start | bytes 4423680 | tf_op jit(solution)/shard_map/all_gather | solution.py:151
  13.3 393.1 %all-gather.19.cloned.1.call-start = ((), (), s32[]{:S(2)}) async-start(), calls=%async_computation.8 | async-start | bytes 2211840 | tf_op jit(solution)/shard_map/all_gather | solution.py:152
  14.2 594.8 %reduce-scatter.7.cloned.1.call-start = ((), (), s32[]{:S(2)}) async-start(), calls=%async_computation.11 | async-start | bytes 1474560 | tf_op jit(solution)/shard_map/reduce_scatter | solution.py:313
  19.6 420.6 %copy-start.53 = (pred[1024]{0:T(1024)(128)(4,1)}, pred[1024]{0:T(1024)(128)(4,1)S(1)}, u32[]{:S(2)}) copy-start(pred[1024]{0:T(1024)(128)(4,1)S(1)} %get-tuple-element.84) | copy-start | bytes 3076
  19.7 420.6 %copy-start.55 = (pred[1024]{0:T(1024)(128)(4,1)}, pred[1024]{0:T(1024)(128)(4,1)S(1)}, u32[]{:S(2)}) copy-start(pred[1024]{0:T(1024)(128)(4,1)S(1)} %get-tuple-element.85) | copy-start | bytes 3076
  32.8 144.1 %copy-start.43 = (f32[768]{0:T(1024)}, f32[768]{0:T(1024)S(1)}, u32[]{:S(2)}) copy-start(f32[768]{0:T(1024)S(1)} %convert_element_type.173) | copy-start | bytes 9220
  33.4 162.2 %copy-start.29 = (f32[1024,32]{0,1:T(8,128)}, f32[1024,32]{0,1:T(8,128)S(1)}, u32[]{:S(2)}) copy-start(f32[1024,32]{0,1:T(8,128)S(1)} %get-tuple-element.86) | copy-start | bytes 393220
  33.4 162.2 %copy-start.31 = (f32[1024,32]{0,1:T(8,128)}, f32[1024,32]{0,1:T(8,128)S(1)}, u32[]{:S(2)}) copy-start(f32[1024,32]{0,1:T(8,128)S(1)} %get-tuple-element.87) | copy-start | bytes 393220
  140.5 182.2 %copy-start.1 = (bf16[1024,768]{0,1:T(8,128)(2,1)}, bf16[1024,768]{0,1:T(8,128)(2,1)S(1)}, u32[]{:S(2)}) copy-start(bf16[1024,768]{0,1:T(8,128)(2,1)S(1)} %copy.68) | copy-start | bytes 4718596
  141.0 35.9 %copy-start.41 = (f32[1024]{0:T(1024)}, f32[1024]{0:T(1024)S(1)}, u32[]{:S(2)}) copy-start(f32[1024]{0:T(1024)S(1)} %broadcast_multiply_fusion.1) | copy-start | bytes 12292
  141.7 35.2 %copy-start.49 = (f32[1024]{0:T(1024)}, f32[1024]{0:T(1024)S(1)}, u32[]{:S(2)}) copy-start(f32[1024]{0:T(1024)S(1)} %fusion.33) | copy-start | bytes 12292
  141.7 35.2 %copy-start.45 = (f32[1024]{0:T(1024)}, f32[1024]{0:T(1024)S(1)}, u32[]{:S(2)}) copy-start(f32[1024]{0:T(1024)S(1)} %fusion.72) | copy-start | bytes 12292
  199.5 10.5 %copy-start.15 = (bf16[1024,12,32]{0,2,1:T(8,128)(2,1)}, bf16[1024,12,32]{0,2,1:T(8,128)(2,1)S(1)}, u32[]{:S(2)}) copy-start(bf16[1024,12,32]{0,2,1:T(8,128)(2,1)S(1)} %get-tuple-element.74) | copy-start | bytes 2359300
  199.5 10.5 %copy-start.17 = (bf16[1024,12,32]{0,2,1:T(8,128)(2,1)}, bf16[1024,12,32]{0,2,1:T(8,128)(2,1)S(1)}, u32[]{:S(2)}) copy-start(bf16[1024,12,32]{0,2,1:T(8,128)(2,1)S(1)} %get-tuple-element.75) | copy-start | bytes 2359300
  199.6 10.5 %copy-start.8 = (bf16[1024,12,32]{0,2,1:T(8,128)(2,1)}, bf16[1024,12,32]{0,2,1:T(8,128)(2,1)S(1)}, u32[]{:S(2)}) copy-start(bf16[1024,12,32]{0,2,1:T(8,128)(2,1)S(1)} %get-tuple-element.82) | copy-start | bytes 2359300
  199.6 10.5 %copy-start.10 = (bf16[1024,12,32]{0,2,1:T(8,128)(2,1)}, bf16[1024,12,32]{0,2,1:T(8,128)(2,1)S(1)}, u32[]{:S(2)}) copy-start(bf16[1024,12,32]{0,2,1:T(8,128)(2,1)S(1)} %get-tuple-element.83) | copy-start | bytes 2359300
  224.6 33.6 %copy-start.24 = (bf16[1024,768]{0,1:T(8,128)(2,1)S(1)}, bf16[1024,768]{0,1:T(8,128)(2,1)}, u32[]{:S(2)}) copy-start(bf16[1024,768]{0,1:T(8,128)(2,1)} %copy.69) | copy-start | bytes 4718596
  308.8 97.6 %copy-start.5 = (bf16[1024,768]{0,1:T(8,128)(2,1)}, bf16[1024,768]{0,1:T(8,128)(2,1)S(1)}, u32[]{:S(2)}) copy-start(bf16[1024,768]{0,1:T(8,128)(2,1)S(1)} %copy.75) | copy-start | bytes 4718596
  406.4 14.5 %copy-start.19 = (f32[1024,2304]{1,0:T(8,128)S(1)}, f32[1024,2304]{1,0:T(8,128)}, u32[]{:S(2)}) copy-start(f32[1024,2304]{1,0:T(8,128)} %fusion.93) | copy-start | bytes 28311556
  420.8 3.5 copy-start.13
  424.4 9.6 copy-start.21
  434.0 3.0 copy-start.22
  434.8 5.4 copy-start.3
  434.9 5.4 copy-start.47
  440.3 3.4 copy-start.26
  449.0 21.1 %copy-start.35 = (bf16[512,768]{0,1:T(8,128)(2,1)}, bf16[512,768]{0,1:T(8,128)(2,1)S(1)}, u32[]{:S(2)}) copy-start(bf16[512,768]{0,1:T(8,128)(2,1)S(1)} %get-tuple-element.78) | copy-start | bytes 2359300
  449.0 21.1 %copy-start.37 = (bf16[512,768]{0,1:T(8,128)(2,1)}, bf16[512,768]{0,1:T(8,128)(2,1)S(1)}, u32[]{:S(2)}) copy-start(bf16[512,768]{0,1:T(8,128)(2,1)S(1)} %get-tuple-element.79) | copy-start | bytes 2359300
  449.0 160.1 %reduce-scatter.11.cloned.1.call-start = ((), (), s32[]{:S(2)}) async-start(), calls=%async_computation.13 | async-start | bytes 2211840 | tf_op jit(solution)/shard_map/reduce_scatter | solution.py:322
  489.3 130.3 %reduce-scatter.9.cloned.1.call-start = ((), (), s32[]{:S(2)}) async-start(), calls=%async_computation.12 | async-start | bytes 4423680 | tf_op jit(solution)/shard_map/reduce_scatter | solution.py:319
  506.3 27.2 %copy-start = (bf16[12,512,1024]{2,1,0:T(8,128)(2,1)}, bf16[12,512,1024]{2,1,0:T(8,128)(2,1)S(1)}, u32[]{:S(2)}) copy-start(bf16[12,512,1024]{2,1,0:T(8,128)(2,1)S(1)} %multiply_convert_fusion.1) | copy-start | bytes 37748740
  506.4 27.2 %copy-start.9 = (bf16[1024,12,32]{0,2,1:T(8,128)(2,1)S(1)}, bf16[1024,12,32]{0,2,1:T(8,128)(2,1)}, u32[]{:S(2)}) copy-start(bf16[1024,12,32]{0,2,1:T(8,128)(2,1)} %copy-done.8) | copy-start | bytes 2359300
  506.4 27.2 %copy-start.11 = (bf16[1024,12,32]{0,2,1:T(8,128)(2,1)S(1)}, bf16[1024,12,32]{0,2,1:T(8,128)(2,1)}, u32[]{:S(2)}) copy-start(bf16[1024,12,32]{0,2,1:T(8,128)(2,1)} %copy-done.10) | copy-start | bytes 2359300
  555.3 7.2 copy-start.14
  572.3 97.4 %reduce-scatter.5.cloned.1.call-start = ((), (), s32[]{:S(2)}) async-start(), calls=%async_computation.10 | async-start | bytes 4423680 | tf_op jit(solution)/shard_map/reduce_scatter | solution.py:310
  577.7 21.4 %copy-start.27 = (bf16[1024,12,64]{0,2,1:T(8,128)(2,1)}, bf16[1024,12,64]{0,2,1:T(8,128)(2,1)S(1)}, u32[]{:S(2)}) copy-start(bf16[1024,12,64]{0,2,1:T(8,128)(2,1)S(1)} %add_convert_fusion.3) | copy-start | bytes 4718596
  577.7 10.7 %copy-start.36 = (bf16[512,768]{0,1:T(8,128)(2,1)S(1)}, bf16[512,768]{0,1:T(8,128)(2,1)}, u32[]{:S(2)}) copy-start(bf16[512,768]{0,1:T(8,128)(2,1)} %copy-done.35) | copy-start | bytes 2359300
  588.4 11.9 %copy-start.2 = (bf16[1024,768]{0,1:T(8,128)(2,1)S(1)}, bf16[1024,768]{0,1:T(8,128)(2,1)}, u32[]{:S(2)}) copy-start(bf16[1024,768]{0,1:T(8,128)(2,1)} %copy-done.1) | copy-start | bytes 4718596
  588.4 11.9 %copy-start.42 = (f32[1024]{0:T(1024)S(1)}, f32[1024]{0:T(1024)}, u32[]{:S(2)}) copy-start(f32[1024]{0:T(1024)} %copy-done.41) | copy-start | bytes 12292
  588.4 11.9 %copy-start.44 = (f32[768]{0:T(1024)S(1)}, f32[768]{0:T(1024)}, u32[]{:S(2)}) copy-start(f32[768]{0:T(1024)} %copy-done.43) | copy-start | bytes 9220
  588.4 11.8 %copy-start.46 = (f32[1024]{0:T(1024)S(1)}, f32[1024]{0:T(1024)}, u32[]{:S(2)}) copy-start(f32[1024]{0:T(1024)} %copy-done.45) | copy-start | bytes 12292
  588.4 11.8 %copy-start.54 = (pred[1024]{0:T(1024)(128)(4,1)S(1)}, pred[1024]{0:T(1024)(128)(4,1)}, u32[]{:S(2)}) copy-start(pred[1024]{0:T(1024)(128)(4,1)} %copy-done.53) | copy-start | bytes 3076
  588.4 11.8 %copy-start.56 = (pred[1024]{0:T(1024)(128)(4,1)S(1)}, pred[1024]{0:T(1024)(128)(4,1)}, u32[]{:S(2)}) copy-start(pred[1024]{0:T(1024)(128)(4,1)} %copy-done.55) | copy-start | bytes 3076
  609.0 131.5 %all-reduce.16.cloned.1.call-start = ((), (), s32[]{:S(2)}) async-start(), calls=%async_computation.16 | async-start | bytes 5013504 | tf_op jit(solution)/shard_map/psum | solution.py:328
  669.7 188.6 %all-gather.23.cloned.1.call-start = ((), (), s32[]{:S(2)}) async-start(), calls=%async_computation.14 | async-start | bytes 14155776 | tf_op jit(solution)/shard_map/all_gather | solution.py:210
  676.4 7.4 copy-start.50
  676.4 299.0 %all-gather.25.cloned.1.call-start = ((), (), s32[]{:S(2)}) async-start(), calls=%async_computation.15 | async-start | bytes 14155776 | tf_op jit(solution)/shard_map/all_gather | solution.py:296
  686.1 3.7 copy-start.52
  686.1 3.7 copy-start.57
  686.1 3.7 copy-start.58
  686.1 3.7 copy-start.61
  740.5 4.4 copy-start.40
  740.5 5.4 copy-start.34
  (17 other events, 30.3 us)
Sparse Core Ops, SparseCore 0:
  9.6 119.4 all-gather.10
  131.5 45.3 all-gather.12
  178.5 116.6 all-gather.20
  297.0 25.7 all-gather.14
  325.0 47.1 all-gather.16
  373.9 32.4 all-gather.18
  449.2 28.7 reduce-scatter.6
  489.4 32.4 reduce-scatter.10
  572.4 47.1 reduce-scatter.8
  622.5 47.1 reduce-scatter.4
  672.4 68.0 all-reduce.15
  742.0 116.3 all-gather.22
  860.5 114.8 all-gather.24
where the time goes:
time: 1030 us; the launch traced here: 1020 us
  waiting for transfers between devices  510 us (50%)
  matrix products  222 us (22%)
  other arithmetic  122 us (12%)
  local copies, waits for them, and re-layouts  113 us (11%)
  blocking collectives  34.9 us (3%)
  between operations  16.4 us (2%)
    all_gather x1, waiting for transfers between devices, on_device(): lax.all_gather(output_dealt[None], 'replica', axis=1, tiled=True)  111 us
    all_gather x1, waiting for transfers between devices, on_device(): lax.all_gather(tokens, 'replica', axis=1, tiled=True)  94.1 us
    all_gather x1, waiting for transfers between devices, on_device(): lax.all_gather(grad_input[None], 'replica', axis=1, tiled=True)  88.9 us
    reduce_scatter x1, waiting for transfers between devices, on_device(): lax.psum_scatter(partial_grads[1].astype(jnp.bfloat16), 'group', scatter_...  50.1 us
    gather x8, local copies, waits for them, and re-layouts, pick_rows(): taken = jnp.take(piece[0], jnp.clip(index_map, 0, piece_rows - 1), axis=0)  49.9 us
    convert_element_type x2, other arithmetic, on_device(): grad_scores = (weights_full * (grad_probs - inner)).astype(jnp.bfloat16)  44.2 us
    all_gather x1, waiting for transfers between devices, on_device(): lax.all_gather(masters[4], 'group', axis=0, tiled=True)  44 us
    dot_general x2, matrix products, on_device(): jnp.einsum('qhd,khd->hqk', grad_block, value_heads, preferred_element_typ...  38.4 us
  transfers between devices with their start and end apart: 13, of which 11 were waited for; matrix products, arithmetic and copies ran while one was open for 36% of the time, Pallas kernels for 0%

commit v1 on v0

v1 whole, which is shorter than its diff:
```python
import functools
import math

import jax
import jax.numpy as jnp
from jax import lax
from jax.experimental import pallas as pl
from jax.experimental.pallas import tpu as pltpu
from jax.sharding import PartitionSpec as P

HEADS = 12
HEAD_DIM = 64
PAIR = 2 * HEAD_DIM
MAX_LENGTH = 768

BLOCK = 256
epsilon = 1e-05
big_negative = -1e30
rope_base = 160000.0

bf16 = jnp.bfloat16
f32 = jnp.float32


def dot_nn(a, b):
    return lax.dot_general(a, b, (((1,), (0,)), ((), ())), preferred_element_type=f32)


def dot_nt(a, b):
    return lax.dot_general(a, b, (((1,), (1,)), ((), ())), preferred_element_type=f32)


def dot_tn(a, b):
    return lax.dot_general(a, b, (((0,), (0,)), ((), ())), preferred_element_type=f32)


def normalized(values):
    centred = values - jnp.mean(values, axis=-1, keepdims=True)
    spread = jnp.mean(centred * centred, axis=-1, keepdims=True)
    scale = lax.rsqrt(spread + epsilon)
    return centred * scale, scale


def turn(values, cosine, sine):
    lane = lax.broadcasted_iota(jnp.int32, values.shape, 1) % HEAD_DIM
    half = HEAD_DIM // 2
    other = jnp.where(
        lane < half, pltpu.roll(values, PAIR - half, 1), pltpu.roll(values, half, 1)
    )
    return values * cosine + other * sine


def params(**kw):
    return pltpu.CompilerParams(vmem_limit_bytes=60 * 1024 * 1024, **kw)


def qkv_body(ahead, own, bounds, x_ref, g_ref, w_ref, cos_ref, sin_ref, n_ref, q_ref, k_ref, v_ref):
    step = pl.program_id(0)
    width = x_ref.shape[1]
    needed = (step >= bounds[0]) & (step < bounds[1])

    @pl.when(needed)
    def _():
        normed, _ = normalized(x_ref[...].astype(f32))
        n1 = (normed * g_ref[...]).astype(bf16)
        n_ref[...] = n1
        cosine = cos_ref[...]
        sine = sin_ref[...]
        keys = dot_nn(n1, w_ref[:, width : 2 * width])
        for at in range(0, width, PAIR):
            k_ref[:, at : at + PAIR] = turn(keys[:, at : at + PAIR], cosine, sine).astype(bf16)
        v_ref[...] = dot_nn(n1, w_ref[:, 2 * width :]).astype(bf16)

        @pl.when((step >= ahead) & (step < ahead + own))
        def _():
            queries = dot_nn(n1, w_ref[:, :width])
            for at in range(0, width, PAIR):
                turned = turn(queries[:, at : at + PAIR], cosine, sine).astype(bf16)
                q_ref[:, at : at + PAIR] = turned * bf16(HEAD_DIM**-0.5)

    @pl.when(jnp.logical_not(needed))
    def _():
        n_ref[...] = jnp.zeros_like(n_ref)
        k_ref[...] = jnp.zeros_like(k_ref)
        v_ref[...] = jnp.zeros_like(v_ref)


def project(bounds, rows, gain, w_qkv, cosine, sine, own_rows):
    total, width = rows.shape
    ahead = MAX_LENGTH // BLOCK
    own = own_rows // BLOCK
    row = lambda i, b: (i, 0)
    whole = lambda i, b: (0, 0)
    own_row = lambda i, b: (jnp.clip(i - ahead, 0, own - 1), 0)
    return pl.pallas_call(
        functools.partial(qkv_body, ahead, own),
        grid_spec=pltpu.PrefetchScalarGridSpec(
            num_scalar_prefetch=1,
            grid=(total // BLOCK,),
            in_specs=[
                pl.BlockSpec((BLOCK, width), row),
                pl.BlockSpec((1, width), whole),
                pl.BlockSpec(w_qkv.shape, whole, pipeline_mode=pl.Buffered(1)),
                pl.BlockSpec((BLOCK, PAIR), row),
                pl.BlockSpec((BLOCK, PAIR), row),
            ],
            out_specs=[
                pl.BlockSpec((BLOCK, width), row),
                pl.BlockSpec((BLOCK, width), own_row),
                pl.BlockSpec((BLOCK, width), row),
                pl.BlockSpec((BLOCK, width), row),
            ],
        ),
        out_shape=[
            jax.ShapeDtypeStruct((total, width), bf16),
            jax.ShapeDtypeStruct((own_rows, width), bf16),
            jax.ShapeDtypeStruct((total, width), bf16),
            jax.ShapeDtypeStruct((total, width), bf16),
        ],
        compiler_params=params(),
        name="project",
    )(bounds, rows, gain, w_qkv, cosine, sine)


def head_lanes(shape, head):
    lane = lax.broadcasted_iota(jnp.int32, shape, 1)
    return lane < HEAD_DIM if head == 0 else lane >= HEAD_DIM


def inside(span_ref, key_row, shape):
    key = lax.broadcasted_iota(jnp.int32, shape, 0) + key_row
    return (key >= span_ref[0:1, :]) & (key < span_ref[1:2, :])


def attend_body(chunks, span_ref, q_ref, k_ref, v_ref, o_ref, lse_ref, acc_ref, top_ref):
    block = pl.program_id(1)
    q_pair = q_ref[...]
    zero = jnp.zeros_like(q_pair)
    queries = [jnp.where(head_lanes(q_pair.shape, h), q_pair, zero) for h in range(2)]
    acc_ref[...] = jnp.zeros_like(acc_ref)
    top_ref[...] = jnp.full_like(top_ref, 2 * big_negative)

    @pl.loop(chunks[block, 0], chunks[block, 1])
    def _(chunk):
        at = pl.multiple_of(chunk * BLOCK, BLOCK)
        keys = k_ref[pl.ds(at, BLOCK), :]
        values = v_ref[pl.ds(at, BLOCK), :]
        ok = inside(span_ref, at, (BLOCK, BLOCK))
        for h in range(2):
            scores = jnp.where(ok, dot_nt(keys, queries[h]), big_negative)
            old_top = top_ref[h : h + 1, :]
            top = jnp.maximum(old_top, jnp.max(scores, axis=0, keepdims=True))
            weights = jnp.exp(scores - top).astype(bf16)
            widened = jnp.where(head_lanes(values.shape, h), values, jnp.ones_like(values))
            acc_ref[h] = acc_ref[h] * jnp.exp(old_top - top) + dot_tn(widened, weights)
            top_ref[h : h + 1, :] = top

    sums = [acc_ref[0, HEAD_DIM : HEAD_DIM + 1, :], acc_ref[1, 0:1, :]]
    both = jnp.concatenate(
        [acc_ref[0, :HEAD_DIM, :] / sums[0], acc_ref[1, HEAD_DIM:, :] / sums[1]], axis=0
    )
    o_ref[...] = both.T.astype(bf16)
    for h in range(2):
        lse_ref[h : h + 1, :] = top_ref[h : h + 1, :] + jnp.log(sums[h])


def attend(chunks, span, q, k, v):
    own_rows, width = q.shape
    total = k.shape[0]
    pairs = width // PAIR
    return pl.pallas_call(
        attend_body,
        grid_spec=pltpu.PrefetchScalarGridSpec(
            num_scalar_prefetch=1,
            grid=(pairs, own_rows // BLOCK),
            in_specs=[
                pl.BlockSpec((8, BLOCK), lambda p, b, c: (0, b)),
                pl.BlockSpec((BLOCK, PAIR), lambda p, b, c: (b, p)),
                pl.BlockSpec((total, PAIR), lambda p, b, c: (0, p)),
                pl.BlockSpec((total, PAIR), lambda p, b, c: (0, p)),
            ],
            out_specs=[
                pl.BlockSpec((BLOCK, PAIR), lambda p, b, c: (b, p)),
                pl.BlockSpec((None, 8, BLOCK), lambda p, b, c: (p, 0, b)),
            ],
            scratch_shapes=[pltpu.VMEM((2, PAIR, BLOCK), f32), pltpu.VMEM((8, BLOCK), f32)],
        ),
        out_shape=[
            jax.ShapeDtypeStruct((own_rows, width), bf16),
            jax.ShapeDtypeStruct((pairs, 8, own_rows), f32),
        ],
        compiler_params=params(),
        name="attend",
    )(chunks, span, q, k, v)


def attend_back_body(
    ahead,
    chunks,
    span_ref,
    q_ref,
    k_ref,
    v_ref,
    o_ref,
    go_ref,
    lse_ref,
    cos_ref,
    sin_ref,
    gq_ref,
    gk_ref,
    gv_ref,
    accq_ref,
    acck_ref,
    accv_ref,
):
    block = pl.program_id(1)

    @pl.when(block == 0)
    def _():
        acck_ref[...] = jnp.zeros_like(acck_ref)
        accv_ref[...] = jnp.zeros_like(accv_ref)

    accq_ref[...] = jnp.zeros_like(accq_ref)
    q_pair = q_ref[...]
    go_pair = go_ref[...]
    zero = jnp.zeros_like(q_pair)
    queries = [jnp.where(head_lanes(q_pair.shape, h), q_pair, zero) for h in range(2)]
    grads = [jnp.where(head_lanes(q_pair.shape, h), go_pair, zero) for h in range(2)]
    products = (o_ref[...].astype(f32) * go_pair.astype(f32)).T
    inner = [
        jnp.sum(products[h * HEAD_DIM : (h + 1) * HEAD_DIM, :], axis=0, keepdims=True)
        for h in range(2)
    ]
    lse = [lse_ref[h : h + 1, :] for h in range(2)]

    @pl.loop(chunks[block, 0], chunks[block, 1])
    def _(chunk):
        at = pl.multiple_of(chunk * BLOCK, BLOCK)
        rows = pl.ds(at, BLOCK)
        keys = k_ref[rows, :]
        values = v_ref[rows, :]
        ok = inside(span_ref, at, (BLOCK, BLOCK))
        grad_k = acck_ref[rows, :]
        grad_v = accv_ref[rows, :]
        for h in range(2):
            scores = jnp.where(ok, dot_nt(keys, queries[h]), big_negative)
            probs = jnp.exp(scores - lse[h])
            grad_probs = dot_nt(values, grads[h])
            grad_v = grad_v + dot_nn(probs.astype(bf16), grads[h])
            grad_scores = (probs * (grad_probs - inner[h])).astype(bf16)
            grad_k = grad_k + dot_nn(grad_scores, queries[h])
            accq_ref[h] = accq_ref[h] + dot_tn(keys, grad_scores)
        acck_ref[rows, :] = grad_k
        accv_ref[rows, :] = grad_v

    both = jnp.concatenate([accq_ref[0, :HEAD_DIM, :], accq_ref[1, HEAD_DIM:, :]], axis=0)
    at = pl.multiple_of((block + ahead) * BLOCK, BLOCK)
    grad_q = both.T * (HEAD_DIM**-0.5)
    gq_ref[...] = turn(
        grad_q, cos_ref[pl.ds(at, BLOCK), :], -sin_ref[pl.ds(at, BLOCK), :]
    ).astype(bf16)

    @pl.when(block == pl.num_programs(1) - 1)
    def _():
        @pl.loop(0, gk_ref.shape[0] // BLOCK)
        def _(part):
            rows = pl.ds(pl.multiple_of(part * BLOCK, BLOCK), BLOCK)
            gk_ref[rows, :] = turn(acck_ref[rows, :], cos_ref[rows, :], -sin_ref[rows, :]).astype(
                bf16
            )
            gv_ref[rows, :] = accv_ref[rows, :].astype(bf16)


def attend_back(chunks, span, q, k, v, o, go, lse, cosine, sine):
    own_rows, width = q.shape
    total = k.shape[0]
    pairs = width // PAIR
    own_spec = pl.BlockSpec((BLOCK, PAIR), lambda p, b, c: (b, p))
    all_spec = pl.BlockSpec((total, PAIR), lambda p, b, c: (0, p))
    fixed = pl.BlockSpec((total, PAIR), lambda p, b, c: (0, 0), pipeline_mode=pl.Buffered(1))
    return pl.pallas_call(
        functools.partial(attend_back_body, MAX_LENGTH // BLOCK),
        grid_spec=pltpu.PrefetchScalarGridSpec(
            num_scalar_prefetch=1,
            grid=(pairs, own_rows // BLOCK),
            in_specs=[
                pl.BlockSpec((8, BLOCK), lambda p, b, c: (0, b)),
                own_spec,
                all_spec,
                all_spec,
                own_spec,
                own_spec,
                pl.BlockSpec((None, 8, BLOCK), lambda p, b, c: (p, 0, b)),
                fixed,
                fixed,
            ],
            out_specs=[own_spec, all_spec, all_spec],
            scratch_shapes=[
                pltpu.VMEM((2, PAIR, BLOCK), f32),
                pltpu.VMEM((total, PAIR), f32),
                pltpu.VMEM((total, PAIR), f32),
            ],
        ),
        out_shape=[
            jax.ShapeDtypeStruct((own_rows, width), bf16),
            jax.ShapeDtypeStruct((total, width), bf16),
            jax.ShapeDtypeStruct((total, width), bf16),
        ],
        compiler_params=params(),
        name="attend_back",
    )(chunks, span, q, k, v, o, go, lse, cosine, sine)


def middle_body(
    o_ref,
    x_ref,
    gy_ref,
    g_ref,
    wo_ref,
    wi_ref,
    wd_ref,
    y_ref,
    n_ref,
    m_ref,
    gu_ref,
    gh_ref,
    go_ref,
    dg_ref,
):
    hidden = wd_ref.shape[0]
    gain = g_ref[...]
    h2 = x_ref[...].astype(f32) + dot_nn(o_ref[...], wo_ref[...])
    normed, scale = normalized(h2)
    n2 = (normed * gain).astype(bf16)
    n_ref[...] = n2
    gate = dot_nn(n2, wi_ref[:, :hidden])
    linear = dot_nn(n2, wi_ref[:, hidden:])
    half_up = 0.5 + 0.5 * lax.erf(gate * math.sqrt(0.5))
    bell = jnp.exp(gate * gate * -0.5) * (1.0 / math.sqrt(2.0 * math.pi))
    activated = gate * half_up
    m = (activated * linear).astype(bf16)
    m_ref[...] = m
    y_ref[...] = (h2 + dot_nn(m, wd_ref[...])).astype(bf16)
    gy = gy_ref[...]
    gm = dot_nt(gy, wd_ref[...])
    ga = (gm * linear * (half_up + gate * bell)).astype(bf16)
    gb = (gm * activated).astype(bf16)
    gu_ref[:, :hidden] = ga
    gu_ref[:, hidden:] = gb
    gn = dot_nt(ga, wi_ref[:, :hidden]) + dot_nt(gb, wi_ref[:, hidden:])

    @pl.when(pl.program_id(0) == 0)
    def _():
        dg_ref[...] = jnp.zeros_like(dg_ref)

    product = gn * normed
    dg_ref[...] += jnp.broadcast_to(jnp.sum(product, axis=0, keepdims=True), dg_ref.shape)
    weighted = gn * gain
    gh2 = gy.astype(f32) + scale * (
        weighted
        - jnp.mean(weighted, axis=-1, keepdims=True)
        - normed * jnp.mean(weighted * normed, axis=-1, keepdims=True)
    )
    ghb = gh2.astype(bf16)
    gh_ref[...] = ghb
    go_ref[...] = dot_nt(ghb, wo_ref[...]).astype(bf16)


def middle(o, x, gy, gain, w_out, w_in, w_down):
    rows, width = x.shape
    hidden = w_down.shape[0]
    row = pl.BlockSpec((BLOCK, width), lambda i: (i, 0))
    whole = lambda a: pl.BlockSpec(a.shape, lambda i: (0, 0), pipeline_mode=pl.Buffered(1))
    wide = lambda n: pl.BlockSpec((BLOCK, n), lambda i: (i, 0))
    shape = lambda n: jax.ShapeDtypeStruct((rows, n), bf16)
    return pl.pallas_call(
        middle_body,
        grid=(rows // BLOCK,),
        in_specs=[row, row, row, whole(gain), whole(w_out), whole(w_in), whole(w_down)],
        out_specs=[
            row,
            row,
            wide(hidden),
            wide(2 * hidden),
            row,
            row,
            pl.BlockSpec((8, width), lambda i: (0, 0)),
        ],
        out_shape=[
            shape(width),
            shape(width),
            shape(hidden),
            shape(2 * hidden),
            shape(width),
            shape(width),
            jax.ShapeDtypeStruct((8, width), f32),
        ],
        compiler_params=params(),
        name="middle",
    )(o, x, gy, gain, w_out, w_in, w_down)


def split_store(product, core, group_count, keep_ref, send_ref):
    half = product.shape[0] // group_count // 2
    for owner in range(group_count):
        at = owner * 2 * half
        lower = product[at : at + half].astype(bf16)
        upper = product[at + half : at + 2 * half].astype(bf16)
        keep_ref[owner * half : (owner + 1) * half, :] = jnp.where(core == 0, lower, upper)
        send_ref[owner * half : (owner + 1) * half, :] = jnp.where(core == 0, upper, lower)


def weight_grad_body(group_count, core, left_ref, right_ref, keep_ref, send_ref):
    split_store(dot_tn(left_ref[...], right_ref[...]), core[0], group_count, keep_ref, send_ref)


def weight_grad(core, left, right, group_count, columns):
    rows, tall = left.shape
    wide = right.shape[1]
    result = pl.BlockSpec((tall // 2, columns), lambda i, c: (0, i))
    return pl.pallas_call(
        functools.partial(weight_grad_body, group_count),
        grid_spec=pltpu.PrefetchScalarGridSpec(
            num_scalar_prefetch=1,
            grid=(wide // columns,),
            in_specs=[
                pl.BlockSpec((rows, tall), lambda i, c: (0, 0), pipeline_mode=pl.Buffered(1)),
                pl.BlockSpec((rows, columns), lambda i, c: (0, i)),
            ],
            out_specs=[result, result],
        ),
        out_shape=[jax.ShapeDtypeStruct((tall // 2, wide), bf16)] * 2,
        compiler_params=params(),
        name="weight_grad",
    )(core, left, right)


def qkv_grad_body(
    ahead, own, group_count, info, n_ref, gq_ref, gk_ref, gv_ref, keep_ref, send_ref, acc_ref
):
    step = pl.program_id(0)
    width = n_ref.shape[1]

    @pl.when(step == 0)
    def _():
        acc_ref[...] = jnp.zeros_like(acc_ref)

    @pl.when((step >= info[0]) & (step < info[1]))
    def _():
        n1 = n_ref[...]
        acc_ref[:, width : 2 * width] += dot_tn(n1, gk_ref[...])
        acc_ref[:, 2 * width :] += dot_tn(n1, gv_ref[...])

        @pl.when((step >= ahead) & (step < ahead + own))
        def _():
            acc_ref[:, :width] += dot_tn(n1, gq_ref[...])

    @pl.when(step == pl.num_programs(0) - 1)
    def _():
        split_store(acc_ref, info[2], group_count, keep_ref, send_ref)


def qkv_grad(info, n1, gq, gk, gv, group_count):
    total, width = n1.shape
    ahead = MAX_LENGTH // BLOCK
    own = gq.shape[0] // BLOCK
    row = pl.BlockSpec((BLOCK, width), lambda i, s: (i, 0))
    own_row = pl.BlockSpec((BLOCK, width), lambda i, s: (jnp.clip(i - ahead, 0, own - 1), 0))
    result = pl.BlockSpec((width // 2, 3 * width), lambda i, s: (0, 0), pipeline_mode=pl.Buffered(1))
    return pl.pallas_call(
        functools.partial(qkv_grad_body, ahead, own, group_count),
        grid_spec=pltpu.PrefetchScalarGridSpec(
            num_scalar_prefetch=1,
            grid=(total // BLOCK,),
            in_specs=[row, own_row, row, row],
            out_specs=[result, result],
            scratch_shapes=[pltpu.VMEM((width, 3 * width), f32)],
        ),
        out_shape=[jax.ShapeDtypeStruct((width // 2, 3 * width), bf16)] * 2,
        compiler_params=params(),
        name="qkv_grad",
    )(info, n1, gq, gk, gv)


def input_grad_body(
    ahead, own, info, x_ref, gq_ref, gk_ref, gv_ref, w_ref, own_ref, before_ref, after_ref, dg_ref
):
    step = pl.program_id(0)
    width = x_ref.shape[1]
    is_own = (step >= ahead) & (step < ahead + own)
    needed = (step >= info[0]) & (step < info[1])

    @pl.when(step == 0)
    def _():
        dg_ref[...] = jnp.zeros_like(dg_ref)

    def count(gn):
        normed, _ = normalized(x_ref[...].astype(f32))
        dg_ref[...] += jnp.broadcast_to(
            jnp.sum(gn * normed, axis=0, keepdims=True), dg_ref.shape
        )

    def shared():
        return dot_nt(gk_ref[...], w_ref[:, width : 2 * width]) + dot_nt(
            gv_ref[...], w_ref[:, 2 * width :]
        )

    @pl.when(is_own)
    def _():
        gn = shared() + dot_nt(gq_ref[...], w_ref[:, :width])
        own_ref[...] = gn
        count(gn)

    for ref, here in ((before_ref, step < ahead), (after_ref, step >= ahead + own)):

        @pl.when(here & needed)
        def _():
            gn = shared()
            ref[...] = gn.astype(bf16)
            count(gn)

        @pl.when(here & jnp.logical_not(needed))
        def _():
            ref[...] = jnp.zeros_like(ref)


def gradient_rows(info, x, gq, gk, gv, w_qkv):
    total, width = x.shape
    ahead = MAX_LENGTH // BLOCK
    own = gq.shape[0] // BLOCK
    row = pl.BlockSpec((BLOCK, width), lambda i, s: (i, 0))
    own_row = pl.BlockSpec((BLOCK, width), lambda i, s: (jnp.clip(i - ahead, 0, own - 1), 0))
    return pl.pallas_call(
        functools.partial(input_grad_body, ahead, own),
        grid_spec=pltpu.PrefetchScalarGridSpec(
            num_scalar_prefetch=1,
            grid=(total // BLOCK,),
            in_specs=[
                row,
                own_row,
                row,
                row,
                pl.BlockSpec(w_qkv.shape, lambda i, s: (0, 0), pipeline_mode=pl.Buffered(1)),
            ],
            out_specs=[
                own_row,
                pl.BlockSpec((BLOCK, width), lambda i, s: (jnp.minimum(i, ahead - 1), 0)),
                pl.BlockSpec((BLOCK, width), lambda i, s: (jnp.maximum(i - ahead - own, 0), 0)),
                pl.BlockSpec((8, width), lambda i, s: (0, 0)),
            ],
        ),
        out_shape=[
            jax.ShapeDtypeStruct((own * BLOCK, width), f32),
            jax.ShapeDtypeStruct((MAX_LENGTH, width), bf16),
            jax.ShapeDtypeStruct((MAX_LENGTH, width), bf16),
            jax.ShapeDtypeStruct((8, width), f32),
        ],
        compiler_params=params(),
        name="gradient_rows",
    )(info, x, gq, gk, gv, w_qkv)


def finish_body(ahead, own, x_ref, gh_ref, gn_ref, before_ref, after_ref, g_ref, out_ref):
    step = pl.program_id(0)
    gn = gn_ref[...]
    gn = gn + jnp.where(step >= own - ahead, before_ref[...].astype(f32), 0.0)
    gn = gn + jnp.where(step < ahead, after_ref[...].astype(f32), 0.0)
    normed, scale = normalized(x_ref[...].astype(f32))
    weighted = gn * g_ref[...]
    out_ref[...] = (
        gh_ref[...].astype(f32)
        + scale
        * (
            weighted
            - jnp.mean(weighted, axis=-1, keepdims=True)
            - normed * jnp.mean(weighted * normed, axis=-1, keepdims=True)
        )
    ).astype(bf16)


def finish(x, gh, gn, before, after, gain):
    rows, width = x.shape
    ahead = MAX_LENGTH // BLOCK
    own = rows // BLOCK
    row = pl.BlockSpec((BLOCK, width), lambda i: (i, 0))
    return pl.pallas_call(
        functools.partial(finish_body, ahead, own),
        grid=(own,),
        in_specs=[
            row,
            row,
            row,
            pl.BlockSpec((BLOCK, width), lambda i: (jnp.maximum(i - own + ahead, 0), 0)),
            pl.BlockSpec((BLOCK, width), lambda i: (jnp.minimum(i, ahead - 1), 0)),
            pl.BlockSpec((1, width), lambda i: (0, 0)),
        ],
        out_specs=row,
        out_shape=jax.ShapeDtypeStruct((rows, width), bf16),
        compiler_params=params(),
        name="finish",
    )(x, gh, gn, before, after, gain)


def swap(values, axis, size, distance):
    return lax.ppermute(values, axis, [(i, i ^ distance) for i in range(size)])


def place_body(group_count, count, info, *refs):
    pieces = refs[:count]
    out_ref, sem = refs[count], refs[count + 1]
    half = out_ref.shape[0] // group_count // 2
    copies = []
    for side in range(2):
        for j in range(group_count):
            source = pieces[side * group_count + j]
            at = (info[0] ^ j) * 2 * half + (info[1] ^ side) * half
            copies.append(
                pltpu.make_async_copy(
                    source.at[pl.ds(0, half), :],
                    out_ref.at[pl.ds(pl.multiple_of(at, half), half), :],
                    sem.at[len(copies)],
                )
            )
    for copy in copies:
        copy.start()
    for copy in copies:
        copy.wait()


def place(info, pieces, group_count, rows):
    any_spec = pl.BlockSpec(memory_space=pl.ANY)
    return pl.pallas_call(
        functools.partial(place_body, group_count, len(pieces)),
        in_specs=[pl.BlockSpec(memory_space=pltpu.SMEM)] + [any_spec] * len(pieces),
        out_specs=any_spec,
        out_shape=jax.ShapeDtypeStruct((rows, pieces[0].shape[1]), pieces[0].dtype),
        scratch_shapes=[pltpu.SemaphoreType.DMA((len(pieces),))],
        name="place",
    )(info, *pieces)


def fetch(half_shard, sizes):
    mine = [half_shard]
    for j in range(1, sizes["group"]):
        mine.append(swap(half_shard, "group", sizes["group"], j))
    return mine + [swap(piece, "replica", sizes["replica"], 1) for piece in mine]


def total(keep, send, group, sizes):
    groups, replicas = sizes["group"], sizes["replica"]
    got = swap(send, "replica", replicas, 1)
    both = (keep.astype(f32) + got.astype(f32)).astype(bf16)
    blocks = both.reshape(groups, both.shape[0] // groups, both.shape[1])
    pick = lambda j: lax.dynamic_index_in_dim(blocks, group ^ j, 0, keepdims=False)
    part = pick(0).astype(f32)
    for j in range(1, groups):
        part = part + swap(pick(j), "group", groups, j).astype(f32)
    distance = 2
    while distance < replicas:
        part = part.astype(bf16)
        part = part.astype(f32) + swap(part, "replica", replicas, distance).astype(f32)
        distance *= 2
    part = part.astype(bf16)
    other = swap(part, "replica", replicas, 1)
    first = lax.axis_index("replica") % 2 == 0
    return jnp.concatenate(
        [jnp.where(first, part, other), jnp.where(first, other, part)], axis=0
    ).astype(f32)


def total_small(values, sizes):
    for axis in ("replica", "group"):
        distance = 1
        while distance < sizes[axis]:
            values = values + swap(values, axis, sizes[axis], distance)
            distance *= 2
    return values


def plan(lengths, base, total_rows, own_rows):
    ends = jnp.cumsum(lengths)
    starts = ends - lengths
    at = base + jnp.arange(total_rows, dtype=jnp.int32)
    in_seq = (at[:, None] >= starts[None, :]) & (at[:, None] < ends[None, :])
    low = jnp.sum(jnp.where(in_seq, starts[None, :], 0), axis=1)
    high = jnp.sum(jnp.where(in_seq, ends[None, :], 0), axis=1)
    return low, high, at - low


def on_device(
    sizes,
    tokens,
    cotangent,
    lengths,
    dealing,
    offsets,
    attn_gain,
    qkv_weight,
    out_weight,
    mlp_gain,
    in_weight,
    down_weight,
):
    own_rows, width = tokens.shape[1:]
    groups, replicas = sizes["group"], sizes["replica"]
    group = lax.axis_index("group")
    replica = lax.axis_index("replica")
    core = replica % 2
    x = tokens[0]
    gy = cotangent[0]

    up = [(i, i + 1) for i in range(replicas - 1)]
    down = [(i + 1, i) for i in range(replicas - 1)]
    rows = jnp.concatenate(
        [
            lax.ppermute(x[own_rows - MAX_LENGTH :], "replica", up),
            x,
            lax.ppermute(x[:MAX_LENGTH], "replica", down),
        ],
        axis=0,
    )
    all_rows = own_rows + 2 * MAX_LENGTH

    gains = jnp.zeros((8, qkv_weight.shape[1]), bf16)
    gains = gains.at[0, : attn_gain.shape[0]].set(attn_gain.astype(bf16))
    gains = gains.at[1, : mlp_gain.shape[0]].set(mlp_gain.astype(bf16))

    def half_of(weight):
        half = weight.shape[0] // 2
        return lax.dynamic_slice_in_dim(weight, core * half, half, 0).astype(bf16)

    where = jnp.stack([group, core]).astype(jnp.int32)
    pieces = fetch(jnp.concatenate([half_of(qkv_weight), gains], axis=0), sizes)
    w_qkv = place(where, pieces, groups, groups * qkv_weight.shape[0])
    shard = attn_gain.shape[0]
    near = jnp.stack([piece[-8:-6, :shard].astype(f32) for piece in pieces[:groups]])
    order = jnp.arange(groups)[:, None] ^ group == jnp.arange(groups)[None, :]
    both_gains = jnp.sum(jnp.where(order[:, :, None, None], near[None], 0.0), axis=1)
    gain_one = both_gains[:, 0].reshape(1, width)
    gain_two = both_gains[:, 1].reshape(1, width)
    w_out = place(where, fetch(half_of(out_weight), sizes), groups, groups * out_weight.shape[0])
    w_in = place(where, fetch(half_of(in_weight), sizes), groups, groups * in_weight.shape[0])
    w_down = place(where, fetch(half_of(down_weight), sizes), groups, groups * down_weight.shape[0])

    base = replica * own_rows - MAX_LENGTH
    low, high, positions = plan(lengths[0], base, all_rows, own_rows)
    own_low = low[MAX_LENGTH : MAX_LENGTH + own_rows] - base
    own_high = high[MAX_LENGTH : MAX_LENGTH + own_rows] - base
    span = jnp.concatenate(
        [own_low[None], own_high[None], jnp.zeros((6, own_rows), jnp.int32)], axis=0
    )
    chunks = jnp.stack(
        [
            own_low.reshape(-1, BLOCK)[:, 0] // BLOCK,
            (own_high.reshape(-1, BLOCK)[:, -1] + BLOCK - 1) // BLOCK,
        ],
        axis=1,
    ).astype(jnp.int32)
    info = jnp.stack([chunks[0, 0], chunks[-1, 1], core]).astype(jnp.int32)

    half_dim = HEAD_DIM // 2
    frequency = jnp.exp(
        -(jnp.arange(half_dim, dtype=f32) * (2.0 / HEAD_DIM)) * math.log(rope_base)
    )
    angles = positions.astype(f32)[:, None] * jnp.tile(frequency, PAIR // half_dim)[None, :]
    sign = jnp.where(jnp.arange(PAIR) % HEAD_DIM < half_dim, -1.0, 1.0).astype(f32)
    cosine = jnp.cos(angles)
    sine = jnp.sin(angles) * sign[None, :]

    n1, q, k, v = project(info, rows, gain_one, w_qkv, cosine, sine, own_rows)
    attended, lse = attend(chunks, span, q, k, v)
    y, n2, m, gu, gh, go, dg_two = middle(attended, x, gy, gain_two, w_out, w_in, w_down)

    core_info = core.reshape(1).astype(jnp.int32)
    down_grad = total(*weight_grad(core_info, m, gy, groups, width // 2), group, sizes)
    in_grad = total(*weight_grad(core_info, n2, gu, groups, width), group, sizes)
    out_grad = total(*weight_grad(core_info, attended, gh, groups, width // 2), group, sizes)

    gq, gk, gv = attend_back(chunks, span, q, k, v, attended, go, lse, cosine, sine)
    qkv_parts = qkv_grad(info, n1, gq, gk, gv, groups)
    gn, before, after, dg_one = gradient_rows(info, rows, gq, gk, gv, w_qkv)
    qkv_sum = total(*qkv_parts, group, sizes)
    before = lax.ppermute(before, "replica", down)
    after = lax.ppermute(after, "replica", up)
    gx = finish(x, gh, gn, before, after, gain_one)

    dg = total_small(jnp.stack([dg_one[0], dg_two[0]]), sizes)
    dg = lax.dynamic_slice_in_dim(dg, group * shard, shard, 1)
    return y[None], gx[None], dg[0], qkv_sum, out_grad, dg[1], in_grad, down_grad


def solution(mesh):
    sizes = dict(mesh.shape)
    return jax.shard_map(
        functools.partial(on_device, sizes),
        mesh=mesh,
        in_specs=(
            P("group", "replica", None),
            P("group", "replica", None),
            P("group", None),
            P("group", None),
            P("group", None, None),
            P("group"),
            P("group", None),
            P("group", None),
            P("group"),
            P("group", None),
            P("group", None),
        ),
        out_specs=(
            P("group", "replica", None),
            P("group", "replica", None),
            P("group"),
            P("group", None),
            P("group", None),
            P("group"),
            P("group", None),
            P("group", None),
        ),
        check_vma=False,
    )
```

time: 1030 us -> 851 us (0.83)
  Pallas kernels: 0 us -> 569 us
  waiting for transfers between devices: 510 us -> 140 us
  matrix products: 222 us -> 0 us
  other arithmetic: 122 us -> 25.8 us
  local copies, waits for them, and re-layouts: 113 us -> 18.5 us
  starting transfers between devices: 0.53 us -> 89.5 us
  blocking collectives: 34.9 us -> 0 us
  between operations: 16.4 us -> 1.39 us
    pallas_call x0 -> x14, Pallas kernels: none -> 569 us  [the longest x4 311 us: place(): pl.pallas_call(functools.partial(place_body, group_count, len(pieces)), i...]
    all_gather x8 -> x0, waiting for transfers between devices: 422 us -> none  [the longest x1 111 us: on_device(): lax.all_gather(output_dealt[None], 'replica', axis=1, tiled=True)]
    dot_general x23 -> x0, matrix products: 207 us -> none  [the longest x2 38.4 us: on_device(): jnp.einsum('qhd,khd->hqk', grad_block, value_heads, preferred_element_typ...]
    ppermute x0 -> x65, waiting for transfers between devices: none -> 140 us  [the longest x61 140 us: swap(): return lax.ppermute(values, axis, [(i, i ^ distance) for i in range(size)])]
    ppermute x0 -> x65, starting transfers between devices: none -> 89.5 us  [the longest x61 80.5 us: swap(): return lax.ppermute(values, axis, [(i, i ^ distance) for i in range(size)])]
    reduce_scatter x4 -> x0, waiting for transfers between devices: 60.7 us -> none  [the longest x1 50.1 us: on_device(): lax.psum_scatter(partial_grads[1].astype(jnp.bfloat16), 'group', scatter_...]
    convert_element_type x21 -> x23, other arithmetic: 63.7 us -> 11 us  [the longest x4 4.47 us: total(): return jnp.concatenate([jnp.where(first, part, other), jnp.where(first, o...]
    gather x8 -> x0, local copies, waits for them, and re-layouts: 49.9 us -> none  [pick_rows(): taken = jnp.take(piece[0], jnp.clip(index_map, 0, piece_rows - 1), axis=0)]
  transfers between devices with their start and end apart: 13 -> 65, of which waited for: 11 -> 22; matrix products, arithmetic and copies ran while one was open for 36% -> 4% of each run, Pallas kernels for 0% -> 53%
where the time goes in v1:
time: 851 us; the launch traced here: 844 us
  Pallas kernels  569 us (67%)
  waiting for transfers between devices  140 us (16%)
  starting transfers between devices  89.5 us (11%)
  other arithmetic  25.8 us (3%)
  local copies, waits for them, and re-layouts  18.5 us (2%)
    pallas_call x4, Pallas kernels, place(): pl.pallas_call(functools.partial(place_body, group_count, len(pieces)), i...  311 us
    ppermute x61, waiting for transfers between devices, swap(): return lax.ppermute(values, axis, [(i, i ^ distance) for i in range(size)])  140 us
    pallas_call x1, Pallas kernels, attend_back(): pl.pallas_call(functools.partial(attend_back_body, MAX_LENGTH // BLOCK),...  86.5 us
    ppermute x61, starting transfers between devices, swap(): return lax.ppermute(values, axis, [(i, i ^ distance) for i in range(size)])  80.5 us
    pallas_call x1, Pallas kernels, attend(): pl.pallas_call(attend_body, grid_spec=pltpu.PrefetchScalarGridSpec(num_sc...  76.5 us
    pallas_call x1, Pallas kernels, middle(): pl.pallas_call(middle_body, grid=(rows // BLOCK,), in_specs=[row, row, ro...  25.4 us
    pallas_call x3, Pallas kernels, weight_grad(): pl.pallas_call(functools.partial(weight_grad_body, group_count), grid_spe...  18.2 us
  transfers between devices with their start and end apart: 65, of which 22 were waited for; matrix products, arithmetic and copies ran while one was open for 4% of the time, Pallas kernels for 53%

profile of v1, /device:TPU:0, one launch (start us, length us, event | category | flops | bytes accessed | tf_op | source)
XLA Modules:
  0.0 844.2 jit_solution(8867077355416682621)
XLA Ops:
  0.7 1.9 dynamic-slice_convert_fusion.2.refs_0_
  2.6 3.0 collective-permute-start.23
  5.6 1.5 collective-permute-start.24
  8.7 2.9 collective-permute-start.11
  14.4 1.5 slice_bitcast_fusion.1
  16.0 1.2 dynamic-slice_convert_fusion.refs_0_
  17.6 6.3 fusion
  27.3 6.7 collective-permute-done.25.refs_3_
  34.5 1.5 collective-permute-start.18
  36.8 1.3 collective-permute-done.15.refs_7_
  38.1 1.5 collective-permute-start.2
  39.6 3.0 collective-permute-done.16.refs_1_
  42.6 12.1 %collective-permute-done.17.refs_2_ = bf16[96,2304]{1,0:T(8,128)(2,1)} collective-permute-done((bf16[96,2304]{1,0:T(8,128)(2,1)S(1)}, bf16[96,2304]{1,0:T(8,128)(2,1)}, u32[]{:S(2)}, u32[]{:S(2)}) %collective-permute-start.17) | collective-permute-done | bytes 442400 | tf_op jit(solution)/shard_map/ppermute | solution.py:605
  55.3 1.5 collective-permute-start.4
  60.3 2.3 collective-permute-start
  62.7 1.3 collective-permute-start.1
  64.0 1.2 pad_add_fusion.1.bounds.info
  65.9 37.6 %place.5.wo_ref = bf16[768,768]{1,0:T(8,128)(2,1)} custom-call(s32[2]{0:T(128)} %pad_add_fusion.2.info, bf16[96,768]{1,0:T(8,128)(2,1)} %copy-done.9, bf16[96,768]{1,0:T(8,128)(2,1)} %collective-permute-done.9.refs_1_, bf16[96,768]{1,0:T(8,128)(2,1)} %collective-permute-done.10.refs_2_, bf16[96,768]{1,0:T(8,128)(2,1)} %collective-permute-done.11.refs_3_, ...), custom_call_target="tpu_custom_call" | custom-call | tf_op jit(solution)/shard_map/place/pallas_call | solution.py:632
  103.5 55.4 %place.7.wd_ref = bf16[1152,768]{1,0:T(8,128)(2,1)} custom-call(s32[2]{0:T(128)} %pad_add_fusion.2.info, bf16[144,768]{1,0:T(8,128)(2,1)} %dynamic-slice_convert_fusion.2.refs_0_, bf16[144,768]{1,0:T(8,128)(2,1)} %collective-permute-done.23.refs_1_, bf16[144,768]{1,0:T(8,128)(2,1)} %collective-permute-done.24.refs_2_, bf16[144,768]{1,0:T(8,128)(2,1)} %copy-done.13, ...), custom_call_target="tpu_custom_call" | custom-call | tf_op jit(solution)/shard_map/place/pallas_call | solution.py:632
  158.9 1.9 collective-permute-start.20
  166.4 109.0 %place.6.wi_ref = bf16[768,2304]{1,0:T(8,128)(2,1)} custom-call(s32[2]{0:T(128)} %pad_add_fusion.2.info, bf16[96,2304]{1,0:T(8,128)(2,1)} %copy-done.4, bf16[96,2304]{1,0:T(8,128)(2,1)} %copy-done.12, bf16[96,2304]{1,0:T(8,128)(2,1)} %collective-permute-done.17.refs_2_, bf16[96,2304]{1,0:T(8,128)(2,1)} %collective-permute-done.18.refs_3_, ...), custom_call_target="tpu_custom_call" | custom-call | tf_op jit(solution)/shard_map/place/pallas_call | solution.py:632
  276.3 109.0 %place.4.w_ref = bf16[768,2304]{1,0:T(8,128)(2,1)} custom-call(s32[2]{0:T(128)} %pad_add_fusion.2.info, bf16[104,2304]{1,0:T(8,128)(2,1)} %copy-done.3, bf16[104,2304]{1,0:T(8,128)(2,1)} %collective-permute-done.2.refs_1_, bf16[104,2304]{1,0:T(8,128)(2,1)} %collective-permute-done.3.refs_2_, bf16[104,2304]{1,0:T(8,128)(2,1)} %collective-permute-done.4.refs_3_, ...), custom_call_target="tpu_custom_call" | custom-call | tf_op jit(solution)/shard_map/place/pallas_call | solution.py:632
  385.4 3.5 pad_maximum_fusion.x_ref
  388.9 16.6 %project.1 = (bf16[2560,768]{1,0:T(8,128)(2,1)}, bf16[1024,768]{1,0:T(8,128)(2,1)}, bf16[2560,768]{1,0:T(8,128)(2,1)}, bf16[2560,768]{1,0:T(8,128)(2,1)}) custom-call(s32[3]{0:T(128)} %pad_add_fusion.1.bounds.info, bf16[2560,768]{1,0:T(8,128)(2,1)} %pad_maximum_fusion.x_ref, f32[1,768]{1,0:T(1,128)} %reshape_squeeze.6.g_ref, bf16[768,2304]{1,0:T(8,128)(2,1)} %place.4.w_ref, ...), custom_call_target="tpu_custom_call" | custom-call | tf_op jit(solution)/shard_map/project/pallas_call | solution.py:95
  405.5 76.5 %attend.1 = (bf16[1024,768]{1,0:T(8,128)(2,1)}, f32[6,8,1024]{2,1,0:T(8,128)}) custom-call(s32[4,2]{1,0:T(4,128)} %pad_add_fusion.chunks, s32[8,1024]{1,0:T(8,128)} %add_add_fusion.span_ref, bf16[1024,768]{1,0:T(8,128)(2,1)} %get-tuple-element.60.q_ref, bf16[2560,768]{1,0:T(8,128)(2,1)} %get-tuple-element.61.k_ref, bf16[2560,768]{1,0:T(8,128)(2,1)} %get-tuple-element.62.v_ref), custom_call_target="tpu_custom_call" | custom-call | tf_op jit(solution)/shard_map/attend/pallas_call | solution.py:171
  481.9 25.4 %middle.1 = (bf16[1024,768]{1,0:T(8,128)(2,1)}, bf16[1024,768]{1,0:T(8,128)(2,1)}, bf16[1024,1152]{1,0:T(8,128)(2,1)}, bf16[1024,2304]{1,0:T(8,128)(2,1)}, bf16[...) custom-call(bf16[1024,768]{1,0:T(8,128)(2,1)} %get-tuple-element.63.o_ref.left_ref, ...), custom_call_target="tpu_custom_call" | custom-call | tf_op jit(solution)/shard_map/middle/pallas_call | solution.py:376
  507.3 4.5 weight_grad.3
  511.9 86.5 %attend_back.1 = (bf16[1024,768]{1,0:T(8,128)(2,1)}, bf16[2560,768]{1,0:T(8,128)(2,1)}, bf16[2560,768]{1,0:T(8,128)(2,1)}) custom-call(s32[4,2]{1,0:T(4,128)} %pad_add_fusion.chunks, s32[8,1024]{1,0:T(8,128)} %add_add_fusion.span_ref, bf16[1024,768]{1,0:T(8,128)(2,1)} %get-tuple-element.60.q_ref, bf16[2560,768]{1,0:T(8,128)(2,1)} %get-tuple-element.61.k_ref, ...), custom_call_target="tpu_custom_call" | custom-call | tf_op jit(solution)/shard_map/attend_back/pallas_call | solution.py:281
  598.4 14.4 %gradient_rows.1 = (f32[1024,768]{1,0:T(8,128)}, bf16[768,768]{1,0:T(8,128)(2,1)}, bf16[768,768]{1,0:T(8,128)(2,1)}, f32[8,768]{1,0:T(8,128)}) custom-call(s32[3]{0:T(128)} %pad_add_fusion.1.bounds.info, bf16[2560,768]{1,0:T(8,128)(2,1)} %pad_maximum_fusion.x_ref, bf16[1024,768]{1,0:T(8,128)(2,1)} %get-tuple-element.68.gq_ref, ...), custom_call_target="tpu_custom_call" | custom-call | tf_op jit(solution)/shard_map/gradient_rows/pallas_call | solution.py:533
  614.4 6.0 weight_grad.5
  620.7 22.6 %collective-permute-start.33 = (f32[2,768]{1,0:T(2,128)S(1)}, f32[2,768]{1,0:T(2,128)S(1)}, u32[]{:S(2)}, u32[]{:S(2)}) collective-permute-start(f32[2,768]{1,0:T(2,128)S(1)} %fusion.20), channel_id=1, source_target_pairs={{0,8},{4,12},{8,0},{12,4},{16,24},{20,28},{24,16},{28,20},{1,9},{5... | collective-permute-start | bytes 18440 | tf_op jit(solution)/shard_map/ppermute | solution.py:605
  644.1 15.3 %collective-permute-start.46 = (bf16[96,768]{1,0:T(8,128)(2,1)}, bf16[96,768]{1,0:T(8,128)(2,1)}, u32[]{:S(2)}, u32[]{:S(2)}) collective-permute-start(bf16[96,768]{1,0:T(8,128)(2,1)} %get-tuple-element.109), channel_id=1, source_target_pairs={{0,2},{1,3},{2,0},{3,1},{4,6},{5,7},{6,4},{7,5},{8,10},{9,11},{10,... | collective-permute-start | bytes 442376 | tf_op jit(solution)/shard_map/ppermute | solution.py:605
  659.6 4.5 collective-permute-done.34
  664.1 1.5 collective-permute-start.35
  665.5 2.2 collective-permute-done.35
  667.7 1.5 collective-permute-start.36
  669.2 13.9 %qkv_grad.1 = (bf16[384,2304]{1,0:T(8,128)(2,1)}, bf16[384,2304]{1,0:T(8,128)(2,1)}) custom-call(s32[3]{0:T(128)} %pad_add_fusion.1.bounds.info, bf16[2560,768]{1,0:T(8,128)(2,1)} %get-tuple-element.76.n_ref, bf16[1024,768]{1,0:T(8,128)(2,1)} %get-tuple-element.68.gq_ref, bf16[2560,768]{1,0:T(8,128)(2,1)} %get-tuple-element.69.gk_ref, ...), custom_call_target="tpu_custom_call" | custom-call | tf_op jit(solution)/shard_map/qkv_grad/pallas_call | solution.py:470
  683.0 7.7 weight_grad.4
  691.5 1.3 collective-permute-start.30
  692.8 4.1 collective-permute-start.31
  696.9 1.1 fusion.12
  698.7 1.6 add_convert_fusion.2
  700.4 2.1 collective-permute-start.59
  703.1 10.0 %collective-permute-done.48 = bf16[96,768]{1,0:T(8,128)(2,1)S(1)} collective-permute-done((bf16[96,768]{1,0:T(8,128)(2,1)S(1)}, bf16[96,768]{1,0:T(8,128)(2,1)S(1)}, u32[]{:S(2)}, u32[]{:S(2)}) %collective-permute-start.48) | collective-permute-done | bytes 147488 | tf_op jit(solution)/shard_map/ppermute | solution.py:605
  713.6 2.9 collective-permute-start.61
  716.6 9.5 %collective-permute-done.60 = bf16[144,768]{1,0:T(8,128)(2,1)S(1)} collective-permute-done((bf16[144,768]{1,0:T(8,128)(2,1)S(1)}, bf16[144,768]{1,0:T(8,128)(2,1)S(1)}, u32[]{:S(2)}, u32[]{:S(2)}) %collective-permute-start.60) | collective-permute-done | bytes 221216 | tf_op jit(solution)/shard_map/ppermute | solution.py:605
  726.8 7.9 collective-permute-done.49
  735.8 6.3 finish.1
  742.2 1.1 collective-permute-start.63
  744.1 11.1 %collective-permute-done.63 = bf16[144,768]{1,0:T(8,128)(2,1)S(1)} collective-permute-done((bf16[144,768]{1,0:T(8,128)(2,1)S(1)}, bf16[144,768]{1,0:T(8,128)(2,1)S(1)}, u32[]{:S(2)}, u32[]{:S(2)}) %collective-permute-start.63) | collective-permute-done | bytes 221216 | tf_op jit(solution)/shard_map/ppermute | solution.py:605
  756.0 2.1 collective-permute-start.52
  759.6 2.0 add_convert_fusion.1
  761.7 2.0 collective-permute-start.38
  765.3 3.8 collective-permute-done.52
  769.1 2.0 collective-permute-start.40
  771.1 9.5 %collective-permute-done.53 = bf16[96,2304]{1,0:T(8,128)(2,1)S(1)} collective-permute-done((bf16[96,2304]{1,0:T(8,128)(2,1)S(1)}, bf16[96,2304]{1,0:T(8,128)(2,1)S(1)}, u32[]{:S(2)}, u32[]{:S(2)}) %collective-permute-start.53) | collective-permute-done | bytes 442400 | tf_op jit(solution)/shard_map/ppermute | solution.py:605
  780.9 7.2 collective-permute-done.38
  788.1 10.7 %collective-permute-done.39 = bf16[96,2304]{1,0:T(8,128)(2,1)S(1)} collective-permute-done((bf16[96,2304]{1,0:T(8,128)(2,1)S(1)}, bf16[96,2304]{1,0:T(8,128)(2,1)S(1)}, u32[]{:S(2)}, u32[]{:S(2)}) %collective-permute-start.39) | collective-permute-done | bytes 442400 | tf_op jit(solution)/shard_map/ppermute | solution.py:605
  799.2 2.1 collective-permute-start.56
  801.3 17.4 %collective-permute-done.41 = bf16[96,2304]{1,0:T(8,128)(2,1)S(1)} collective-permute-done((bf16[96,2304]{1,0:T(8,128)(2,1)S(1)}, bf16[96,2304]{1,0:T(8,128)(2,1)S(1)}, u32[]{:S(2)}, u32[]{:S(2)}) %collective-permute-start.41) | collective-permute-done | bytes 442400 | tf_op jit(solution)/shard_map/ppermute | solution.py:605
  819.3 11.4 %collective-permute-done.56 = bf16[96,2304]{1,0:T(8,128)(2,1)S(1)} collective-permute-done((bf16[96,2304]{1,0:T(8,128)(2,1)S(1)}, bf16[96,2304]{1,0:T(8,128)(2,1)S(1)}, u32[]{:S(2)}, u32[]{:S(2)}) %collective-permute-start.56) | collective-permute-done | bytes 442400 | tf_op jit(solution)/shard_map/ppermute | solution.py:605
  830.9 9.2 %collective-permute-done.42 = bf16[96,2304]{1,0:T(8,128)(2,1)S(1)} collective-permute-done((bf16[96,2304]{1,0:T(8,128)(2,1)S(1)}, bf16[96,2304]{1,0:T(8,128)(2,1)S(1)}, u32[]{:S(2)}, u32[]{:S(2)}) %collective-permute-start.42) | collective-permute-done | bytes 442400 | tf_op jit(solution)/shard_map/ppermute | solution.py:605
  840.4 1.3 maximum_convert_fusion.1
  842.1 1.3 maximum_convert_fusion
  (216 shorter events, 35.7 us)
Async XLA Ops:
  2.6 24.1 %collective-permute-start.23 = (bf16[144,768]{1,0:T(8,128)(2,1)}, bf16[144,768]{1,0:T(8,128)(2,1)}, u32[]{:S(2)}, u32[]{:S(2)}) collective-permute-start(bf16[144,768]{1,0:T(8,128)(2,1)} %dynamic-slice_convert_fusion.2.refs_0_), channel_id=1, source_target_pairs={{0,1},{1,0},{2,3},{3,2},{4,5},{5,4},{6,7},{7,6},{8,9},{9,8},{10,11... | collective-permute-start | bytes 663560 | tf_op jit(solution)/shard_map/ppermute | solution.py:605
  5.6 21.2 %collective-permute-start.24 = (bf16[144,768]{1,0:T(8,128)(2,1)}, bf16[144,768]{1,0:T(8,128)(2,1)}, u32[]{:S(2)}, u32[]{:S(2)}) collective-permute-start(bf16[144,768]{1,0:T(8,128)(2,1)} %dynamic-slice_convert_fusion.2.refs_0_), channel_id=1, source_target_pairs={{0,2},{1,3},{2,0},{3,1},{4,6},{5,7},{6,4},{7,5},{8,10},{9,11},{10,... | collective-permute-start | bytes 663560 | tf_op jit(solution)/shard_map/ppermute | solution.py:605
  8.1 16.4 %collective-permute-start.9 = (bf16[96,768]{1,0:T(8,128)(2,1)S(1)}, bf16[96,768]{1,0:T(8,128)(2,1)}, u32[]{:S(2)}, u32[]{:S(2)}) collective-permute-start(bf16[96,768]{1,0:T(8,128)(2,1)S(1)} %dynamic-slice_convert_fusion.3.refs_0_), channel_id=1, source_target_pairs={{0,1},{1,0},{2,3},{3,2},{4,5},{5,4},{6,7},{7,6},{8,9},{9,8},{10,11... | collective-permute-start | bytes 442376 | tf_op jit(solution)/shard_map/ppermute | solution.py:605
  8.7 15.8 %collective-permute-start.10 = (bf16[96,768]{1,0:T(8,128)(2,1)S(1)}, bf16[96,768]{1,0:T(8,128)(2,1)}, u32[]{:S(2)}, u32[]{:S(2)}) collective-permute-start(bf16[96,768]{1,0:T(8,128)(2,1)S(1)} %dynamic-slice_convert_fusion.3.refs_0_), channel_id=1, source_target_pairs={{0,2},{1,3},{2,0},{3,1},{4,6},{5,7},{6,4},{7,5},{8,10},{9,11},{10,... | collective-permute-start | bytes 442376 | tf_op jit(solution)/shard_map/ppermute | solution.py:605
  8.7 15.9 %collective-permute-start.11 = (bf16[96,768]{1,0:T(8,128)(2,1)S(1)}, bf16[96,768]{1,0:T(8,128)(2,1)}, u32[]{:S(2)}, u32[]{:S(2)}) collective-permute-start(bf16[96,768]{1,0:T(8,128)(2,1)S(1)} %dynamic-slice_convert_fusion.3.refs_0_), channel_id=1, source_target_pairs={{0,3},{1,2},{2,1},{3,0},{4,7},{5,6},{6,5},{7,4},{8,11},{9,10},{10,... | collective-permute-start | bytes 442376 | tf_op jit(solution)/shard_map/ppermute | solution.py:605
  24.5 9.5 %collective-permute-start.25 = (bf16[144,768]{1,0:T(8,128)(2,1)}, bf16[144,768]{1,0:T(8,128)(2,1)S(1)}, u32[]{:S(2)}, u32[]{:S(2)}) collective-permute-start(bf16[144,768]{1,0:T(8,128)(2,1)} %dynamic-slice_convert_fusion.2.refs_0_), channel_id=1, source_target_pairs={{0,3},{1,2},{2,1},{3,0},{4,7},{5,6},{6,5},{7,4},{8,11},{9,10},{10,... | collective-permute-start | bytes 663560 | tf_op jit(solution)/shard_map/ppermute | solution.py:605
  24.6 9.9 %collective-permute-start.26 = (bf16[144,768]{1,0:T(8,128)(2,1)}, bf16[144,768]{1,0:T(8,128)(2,1)S(1)}, u32[]{:S(2)}, u32[]{:S(2)}) collective-permute-start(bf16[144,768]{1,0:T(8,128)(2,1)} %dynamic-slice_convert_fusion.2.refs_0_), channel_id=1, source_target_pairs={{0,4},{4,0},{8,12},{12,8},{16,20},{20,16},{24,28},{28,24},{1,5},{5... | collective-permute-start | bytes 663560 | tf_op jit(solution)/shard_map/ppermute | solution.py:605
  25.9 16.7 %collective-permute-start.16 = (bf16[96,2304]{1,0:T(8,128)(2,1)S(1)}, bf16[96,2304]{1,0:T(8,128)(2,1)S(1)}, u32[]{:S(2)}, u32[]{:S(2)}) collective-permute-start(bf16[96,2304]{1,0:T(8,128)(2,1)S(1)} %dynamic-slice_convert_fusion.refs_0_), channel_id=1, source_target_pairs={{0,1},{1,0},{2,3},{3,2},{4,5},{5,4},{6,7},{7,6},{8,9},{9,8},{10,11... | collective-permute-start | bytes 1327112 | tf_op jit(solution)/shard_map/ppermute | solution.py:605
  26.7 9.3 %collective-permute-start.13 = (bf16[96,768]{1,0:T(8,128)(2,1)}, bf16[96,768]{1,0:T(8,128)(2,1)S(1)}, u32[]{:S(2)}, u32[]{:S(2)}) collective-permute-start(bf16[96,768]{1,0:T(8,128)(2,1)} %collective-permute-done.9.refs_1_), channel_id=1, source_target_pairs={{0,4},{4,0},{8,12},{12,8},{16,20},{20,16},{24,28},{28,24},{1,5},{5... | collective-permute-start | bytes 442376 | tf_op jit(solution)/shard_map/ppermute | solution.py:605
  26.8 9.3 %collective-permute-start.14 = (bf16[96,768]{1,0:T(8,128)(2,1)}, bf16[96,768]{1,0:T(8,128)(2,1)S(1)}, u32[]{:S(2)}, u32[]{:S(2)}) collective-permute-start(bf16[96,768]{1,0:T(8,128)(2,1)} %collective-permute-done.10.refs_2_), channel_id=1, source_target_pairs={{0,4},{4,0},{8,12},{12,8},{16,20},{20,16},{24,28},{28,24},{1,5},{5... | collective-permute-start | bytes 442376 | tf_op jit(solution)/shard_map/ppermute | solution.py:605
  34.0 20.7 %collective-permute-start.17 = (bf16[96,2304]{1,0:T(8,128)(2,1)S(1)}, bf16[96,2304]{1,0:T(8,128)(2,1)}, u32[]{:S(2)}, u32[]{:S(2)}) collective-permute-start(bf16[96,2304]{1,0:T(8,128)(2,1)S(1)} %dynamic-slice_convert_fusion.refs_0_), channel_id=1, source_target_pairs={{0,2},{1,3},{2,0},{3,1},{4,6},{5,7},{6,4},{7,5},{8,10},{9,11},{10,... | collective-permute-start | bytes 1327112 | tf_op jit(solution)/shard_map/ppermute | solution.py:605
  34.5 20.2 %collective-permute-start.18 = (bf16[96,2304]{1,0:T(8,128)(2,1)S(1)}, bf16[96,2304]{1,0:T(8,128)(2,1)}, u32[]{:S(2)}, u32[]{:S(2)}) collective-permute-start(bf16[96,2304]{1,0:T(8,128)(2,1)S(1)} %dynamic-slice_convert_fusion.refs_0_), channel_id=1, source_target_pairs={{0,3},{1,2},{2,1},{3,0},{4,7},{5,6},{6,5},{7,4},{8,11},{9,10},{10,... | collective-permute-start | bytes 1327112 | tf_op jit(solution)/shard_map/ppermute | solution.py:605
  36.0 19.3 %collective-permute-start.19 = (bf16[96,2304]{1,0:T(8,128)(2,1)S(1)}, bf16[96,2304]{1,0:T(8,128)(2,1)}, u32[]{:S(2)}, u32[]{:S(2)}) collective-permute-start(bf16[96,2304]{1,0:T(8,128)(2,1)S(1)} %dynamic-slice_convert_fusion.refs_0_), channel_id=1, source_target_pairs={{0,4},{4,0},{8,12},{12,8},{16,20},{20,16},{24,28},{28,24},{1,5},{5... | collective-permute-start | bytes 1327112 | tf_op jit(solution)/shard_map/ppermute | solution.py:605
  36.1 2.0 collective-permute-start.15
  38.1 24.6 %collective-permute-start.2 = (bf16[104,2304]{1,0:T(8,128)(2,1)S(1)}, bf16[104,2304]{1,0:T(8,128)(2,1)}, u32[]{:S(2)}, u32[]{:S(2)}) collective-permute-start(bf16[104,2304]{1,0:T(8,128)(2,1)S(1)} %pad_maximum_fusion.1.refs_0_), channel_id=1, source_target_pairs={{0,1},{1,0},{2,3},{3,2},{4,5},{5,4},{6,7},{7,6},{8,9},{9,8},{10,11... | collective-permute-start | bytes 1437704 | tf_op jit(solution)/shard_map/ppermute | solution.py:605
  42.5 14.2 %collective-permute-start.27 = (bf16[144,768]{1,0:T(8,128)(2,1)}, bf16[144,768]{1,0:T(8,128)(2,1)}, u32[]{:S(2)}, u32[]{:S(2)}) collective-permute-start(bf16[144,768]{1,0:T(8,128)(2,1)} %collective-permute-done.23.refs_1_), channel_id=1, source_target_pairs={{0,4},{4,0},{8,12},{12,8},{16,20},{20,16},{24,28},{28,24},{1,5},{5... | collective-permute-start | bytes 663560 | tf_op jit(solution)/shard_map/ppermute | solution.py:605
  54.7 3.3 collective-permute-start.28
  54.7 104.2 %collective-permute-start.3 = (bf16[104,2304]{1,0:T(8,128)(2,1)S(1)}, bf16[104,2304]{1,0:T(8,128)(2,1)}, u32[]{:S(2)}, u32[]{:S(2)}) collective-permute-start(bf16[104,2304]{1,0:T(8,128)(2,1)S(1)} %pad_maximum_fusion.1.refs_0_), channel_id=1, source_target_pairs={{0,2},{1,3},{2,0},{3,1},{4,6},{5,7},{6,4},{7,5},{8,10},{9,11},{10,... | collective-permute-start | bytes 1437704 | tf_op jit(solution)/shard_map/ppermute | solution.py:605
  55.3 105.6 %collective-permute-start.4 = (bf16[104,2304]{1,0:T(8,128)(2,1)S(1)}, bf16[104,2304]{1,0:T(8,128)(2,1)}, u32[]{:S(2)}, u32[]{:S(2)}) collective-permute-start(bf16[104,2304]{1,0:T(8,128)(2,1)S(1)} %pad_maximum_fusion.1.refs_0_), channel_id=1, source_target_pairs={{0,3},{1,2},{2,1},{3,0},{4,7},{5,6},{6,5},{7,4},{8,11},{9,10},{10,... | collective-permute-start | bytes 1437704 | tf_op jit(solution)/shard_map/ppermute | solution.py:605
  56.8 104.2 %collective-permute-start.5 = (bf16[104,2304]{1,0:T(8,128)(2,1)S(1)}, bf16[104,2304]{1,0:T(8,128)(2,1)}, u32[]{:S(2)}, u32[]{:S(2)}) collective-permute-start(bf16[104,2304]{1,0:T(8,128)(2,1)S(1)} %pad_maximum_fusion.1.refs_0_), channel_id=1, source_target_pairs={{0,4},{4,0},{8,12},{12,8},{16,20},{20,16},{24,28},{28,24},{1,5},{5... | collective-permute-start | bytes 1437704 | tf_op jit(solution)/shard_map/ppermute | solution.py:605
  58.0 1.6 collective-permute-start.29
  60.3 325.0 %collective-permute-start = (bf16[768,768]{1,0:T(8,128)(2,1)}, bf16[768,768]{1,0:T(8,128)(2,1)S(1)}, u32[]{:S(2)}, u32[]{:S(2)}) collective-permute-start(bf16[768,768]{1,0:T(8,128)(2,1)} %get-tuple-element.98), channel_id=1, source_target_pairs={{0,4},{4,8},{8,12},{12,16},{16,20},{20,24},{24,28},{1,5},{5,9},{9,... | collective-permute-start | bytes 3538952 | tf_op jit(solution)/shard_map/ppermute | solution.py:716
  62.7 322.7 %collective-permute-start.1 = (bf16[768,768]{1,0:T(8,128)(2,1)}, bf16[768,768]{1,0:T(8,128)(2,1)}, u32[]{:S(2)}, u32[]{:S(2)}) collective-permute-start(bf16[768,768]{1,0:T(8,128)(2,1)} %get-tuple-element.99), channel_id=1, source_target_pairs={{4,0},{8,4},{12,8},{16,12},{20,16},{24,20},{28,24},{5,1},{9,5},{13... | collective-permute-start | bytes 3538952 | tf_op jit(solution)/shard_map/ppermute | solution.py:718
  158.9 3.8 collective-permute-start.20
  160.9 2.4 collective-permute-start.21
  161.0 2.9 collective-permute-start.22
  162.8 112.8 %collective-permute-start.7 = (bf16[104,2304]{1,0:T(8,128)(2,1)}, bf16[104,2304]{1,0:T(8,128)(2,1)S(1)}, u32[]{:S(2)}, u32[]{:S(2)}) collective-permute-start(bf16[104,2304]{1,0:T(8,128)(2,1)} %collective-permute-done.3.refs_2_), channel_id=1, source_target_pairs={{0,4},{4,0},{8,12},{12,8},{16,20},{20,16},{24,28},{28,24},{1,5},{5... | collective-permute-start | bytes 1437704 | tf_op jit(solution)/shard_map/ppermute | solution.py:605
  163.3 112.3 %collective-permute-start.8 = (bf16[104,2304]{1,0:T(8,128)(2,1)}, bf16[104,2304]{1,0:T(8,128)(2,1)}, u32[]{:S(2)}, u32[]{:S(2)}) collective-permute-start(bf16[104,2304]{1,0:T(8,128)(2,1)} %collective-permute-done.4.refs_3_), channel_id=1, source_target_pairs={{0,4},{4,0},{8,12},{12,8},{16,20},{20,16},{24,28},{28,24},{1,5},{5... | collective-permute-start | bytes 1437704 | tf_op jit(solution)/shard_map/ppermute | solution.py:605
  163.9 111.6 %collective-permute-start.6 = (bf16[104,2304]{1,0:T(8,128)(2,1)}, bf16[104,2304]{1,0:T(8,128)(2,1)}, u32[]{:S(2)}, u32[]{:S(2)}) collective-permute-start(bf16[104,2304]{1,0:T(8,128)(2,1)} %collective-permute-done.2.refs_1_), channel_id=1, source_target_pairs={{0,4},{4,0},{8,12},{12,8},{16,20},{20,16},{24,28},{28,24},{1,5},{5... | collective-permute-start | bytes 1437704 | tf_op jit(solution)/shard_map/ppermute | solution.py:605
  511.9 131.4 %collective-permute-start.44 = (bf16[384,768]{1,0:T(8,128)(2,1)}, bf16[384,768]{1,0:T(8,128)(2,1)S(1)}, u32[]{:S(2)}, u32[]{:S(2)}) collective-permute-start(bf16[384,768]{1,0:T(8,128)(2,1)} %get-tuple-element.80), channel_id=1, source_target_pairs={{0,4},{4,0},{8,12},{12,8},{16,20},{20,16},{24,28},{28,24},{1,5},{5... | collective-permute-start | bytes 1769480 | tf_op jit(solution)/shard_map/ppermute | solution.py:605
  614.3 6.4 collective-permute-start.32
  620.4 78.3 %collective-permute-start.58 = (bf16[576,768]{1,0:T(8,128)(2,1)}, bf16[576,768]{1,0:T(8,128)(2,1)}, u32[]{:S(2)}, u32[]{:S(2)}) collective-permute-start(bf16[576,768]{1,0:T(8,128)(2,1)} %get-tuple-element.87), channel_id=1, source_target_pairs={{0,4},{4,0},{8,12},{12,8},{16,20},{20,16},{24,28},{28,24},{1,5},{5... | collective-permute-start | bytes 2654216 | tf_op jit(solution)/shard_map/ppermute | solution.py:605
  620.7 38.8 %collective-permute-start.33 = (f32[2,768]{1,0:T(2,128)S(1)}, f32[2,768]{1,0:T(2,128)S(1)}, u32[]{:S(2)}, u32[]{:S(2)}) collective-permute-start(f32[2,768]{1,0:T(2,128)S(1)} %fusion.20), channel_id=1, source_target_pairs={{0,8},{4,12},{8,0},{12,4},{16,24},{20,28},{24,16},{28,20},{1,9},{5... | collective-permute-start | bytes 18440 | tf_op jit(solution)/shard_map/ppermute | solution.py:605
  644.1 46.7 %collective-permute-start.45 = (bf16[96,768]{1,0:T(8,128)(2,1)S(1)}, bf16[96,768]{1,0:T(8,128)(2,1)S(1)}, u32[]{:S(2)}, u32[]{:S(2)}) collective-permute-start(bf16[96,768]{1,0:T(8,128)(2,1)S(1)} %get-tuple-element.107), channel_id=1, source_target_pairs={{0,1},{1,0},{2,3},{3,2},{4,5},{5,4},{6,7},{7,6},{8,9},{9,8},{10,11... | collective-permute-start | bytes 442376 | tf_op jit(solution)/shard_map/ppermute | solution.py:605
  644.1 48.7 %collective-permute-start.46 = (bf16[96,768]{1,0:T(8,128)(2,1)}, bf16[96,768]{1,0:T(8,128)(2,1)}, u32[]{:S(2)}, u32[]{:S(2)}) collective-permute-start(bf16[96,768]{1,0:T(8,128)(2,1)} %get-tuple-element.109), channel_id=1, source_target_pairs={{0,2},{1,3},{2,0},{3,1},{4,6},{5,7},{6,4},{7,5},{8,10},{9,11},{10,... | collective-permute-start | bytes 442376 | tf_op jit(solution)/shard_map/ppermute | solution.py:605
  659.5 37.4 %collective-permute-start.47 = (bf16[96,768]{1,0:T(8,128)(2,1)}, bf16[96,768]{1,0:T(8,128)(2,1)}, u32[]{:S(2)}, u32[]{:S(2)}) collective-permute-start(bf16[96,768]{1,0:T(8,128)(2,1)} %get-tuple-element.108), channel_id=1, source_target_pairs={{0,3},{1,2},{2,1},{3,0},{4,7},{5,6},{6,5},{7,4},{8,11},{9,10},{10,... | collective-permute-start | bytes 442376 | tf_op jit(solution)/shard_map/ppermute | solution.py:605
  659.5 4.6 collective-permute-start.34
  664.1 3.6 collective-permute-start.35
  667.7 23.0 %collective-permute-start.36 = (f32[2,768]{1,0:T(2,128)S(1)}, f32[2,768]{1,0:T(2,128)S(1)}, u32[]{:S(2)}, u32[]{:S(2)}) collective-permute-start(f32[2,768]{1,0:T(2,128)S(1)} %add.185), channel_id=1, source_target_pairs={{0,2},{1,3},{2,0},{3,1},{4,6},{5,7},{6,4},{7,5},{8,10},{9,11},{10,... | collective-permute-start | bytes 18440 | tf_op jit(solution)/shard_map/ppermute | solution.py:605
  690.7 64.6 %collective-permute-start.51 = (bf16[384,2304]{1,0:T(8,128)(2,1)}, bf16[384,2304]{1,0:T(8,128)(2,1)S(1)}, u32[]{:S(2)}, u32[]{:S(2)}) collective-permute-start(bf16[384,2304]{1,0:T(8,128)(2,1)} %get-tuple-element.84), channel_id=1, source_target_pairs={{0,4},{4,0},{8,12},{12,8},{16,20},{20,16},{24,28},{28,24},{1,5},{5... | collective-permute-start | bytes 5308424 | tf_op jit(solution)/shard_map/ppermute | solution.py:605
  691.5 43.3 %collective-permute-start.30 = (bf16[768,768]{1,0:T(8,128)(2,1)}, bf16[768,768]{1,0:T(8,128)(2,1)S(1)}, u32[]{:S(2)}, u32[]{:S(2)}) collective-permute-start(bf16[768,768]{1,0:T(8,128)(2,1)} %get-tuple-element.72), channel_id=1, source_target_pairs={{4,0},{8,4},{12,8},{16,12},{20,16},{24,20},{28,24},{5,1},{9,5},{13... | collective-permute-start | bytes 3538952 | tf_op jit(solution)/shard_map/ppermute | solution.py:783
  692.8 42.1 %collective-permute-start.31 = (bf16[768,768]{1,0:T(8,128)(2,1)}, bf16[768,768]{1,0:T(8,128)(2,1)}, u32[]{:S(2)}, u32[]{:S(2)}) collective-permute-start(bf16[768,768]{1,0:T(8,128)(2,1)} %get-tuple-element.73), channel_id=1, source_target_pairs={{0,4},{4,8},{8,12},{12,16},{16,20},{20,24},{24,28},{1,5},{5,9},{9,... | collective-permute-start | bytes 3538952 | tf_op jit(solution)/shard_map/ppermute | solution.py:784
  698.0 15.0 %collective-permute-start.48 = (bf16[96,768]{1,0:T(8,128)(2,1)S(1)}, bf16[96,768]{1,0:T(8,128)(2,1)S(1)}, u32[]{:S(2)}, u32[]{:S(2)}) collective-permute-start(bf16[96,768]{1,0:T(8,128)(2,1)S(1)} %fusion.12), channel_id=1, source_target_pairs={{0,8},{4,12},{8,0},{12,4},{16,24},{20,28},{24,16},{28,20},{1,9},{5... | collective-permute-start | bytes 442376 | tf_op jit(solution)/shard_map/ppermute | solution.py:605
  700.4 13.2 %collective-permute-start.59 = (bf16[144,768]{1,0:T(8,128)(2,1)S(1)}, bf16[144,768]{1,0:T(8,128)(2,1)S(1)}, u32[]{:S(2)}, u32[]{:S(2)}) collective-permute-start(bf16[144,768]{1,0:T(8,128)(2,1)S(1)} %get-tuple-element.100), channel_id=1, source_target_pairs={{0,1},{1,0},{2,3},{3,2},{4,5},{5,4},{6,7},{7,6},{8,9},{9,8},{10,11... | collective-permute-start | bytes 663560 | tf_op jit(solution)/shard_map/ppermute | solution.py:605
  713.1 13.0 %collective-permute-start.60 = (bf16[144,768]{1,0:T(8,128)(2,1)S(1)}, bf16[144,768]{1,0:T(8,128)(2,1)S(1)}, u32[]{:S(2)}, u32[]{:S(2)}) collective-permute-start(bf16[144,768]{1,0:T(8,128)(2,1)S(1)} %get-tuple-element.102), channel_id=1, source_target_pairs={{0,2},{1,3},{2,0},{3,1},{4,6},{5,7},{6,4},{7,5},{8,10},{9,11},{10,... | collective-permute-start | bytes 663560 | tf_op jit(solution)/shard_map/ppermute | solution.py:605
  713.6 12.5 %collective-permute-start.61 = (bf16[144,768]{1,0:T(8,128)(2,1)S(1)}, bf16[144,768]{1,0:T(8,128)(2,1)S(1)}, u32[]{:S(2)}, u32[]{:S(2)}) collective-permute-start(bf16[144,768]{1,0:T(8,128)(2,1)S(1)} %get-tuple-element.101), channel_id=1, source_target_pairs={{0,3},{1,2},{2,1},{3,0},{4,7},{5,6},{6,5},{7,4},{8,11},{9,10},{10,... | collective-permute-start | bytes 663560 | tf_op jit(solution)/shard_map/ppermute | solution.py:605
  726.1 33.6 %collective-permute-start.37 = (bf16[384,2304]{1,0:T(8,128)(2,1)}, bf16[384,2304]{1,0:T(8,128)(2,1)}, u32[]{:S(2)}, u32[]{:S(2)}) collective-permute-start(bf16[384,2304]{1,0:T(8,128)(2,1)} %get-tuple-element.78), channel_id=1, source_target_pairs={{0,4},{4,0},{8,12},{12,8},{16,20},{20,16},{24,28},{28,24},{1,5},{5... | collective-permute-start | bytes 5308424 | tf_op jit(solution)/shard_map/ppermute | solution.py:605
  726.2 8.6 %collective-permute-start.49 = (bf16[96,768]{1,0:T(8,128)(2,1)S(1)}, bf16[96,768]{1,0:T(8,128)(2,1)S(1)}, u32[]{:S(2)}, u32[]{:S(2)}) collective-permute-start(bf16[96,768]{1,0:T(8,128)(2,1)S(1)} %add_convert_fusion.11), channel_id=1, source_target_pairs={{0,16},{4,20},{8,24},{12,28},{16,0},{20,4},{24,8},{28,12},{1,17},{... | collective-permute-start | bytes 442376 | tf_op jit(solution)/shard_map/ppermute | solution.py:605
  734.7 7.4 collective-permute-start.62
  734.8 8.5 %collective-permute-start.50 = (bf16[96,768]{1,0:T(8,128)(2,1)S(1)}, bf16[96,768]{1,0:T(8,128)(2,1)S(1)}, u32[]{:S(2)}, u32[]{:S(2)}) collective-permute-start(bf16[96,768]{1,0:T(8,128)(2,1)S(1)} %add_convert_fusion.10), channel_id=1, source_target_pairs={{0,4},{4,0},{8,12},{12,8},{16,20},{20,16},{24,28},{28,24},{1,5},{5... | collective-permute-start | bytes 442376 | tf_op jit(solution)/shard_map/ppermute | solution.py:605
  742.2 13.1 %collective-permute-start.63 = (bf16[144,768]{1,0:T(8,128)(2,1)S(1)}, bf16[144,768]{1,0:T(8,128)(2,1)S(1)}, u32[]{:S(2)}, u32[]{:S(2)}) collective-permute-start(bf16[144,768]{1,0:T(8,128)(2,1)S(1)} %add_convert_fusion.9), channel_id=1, source_target_pairs={{0,16},{4,20},{8,24},{12,28},{16,0},{20,4},{24,8},{28,12},{1,17},{... | collective-permute-start | bytes 663560 | tf_op jit(solution)/shard_map/ppermute | solution.py:605
  755.3 8.4 collective-permute-start.64
  756.0 13.1 %collective-permute-start.52 = (bf16[96,2304]{1,0:T(8,128)(2,1)S(1)}, bf16[96,2304]{1,0:T(8,128)(2,1)S(1)}, u32[]{:S(2)}, u32[]{:S(2)}) collective-permute-start(bf16[96,2304]{1,0:T(8,128)(2,1)S(1)} %get-tuple-element.92), channel_id=1, source_target_pairs={{0,1},{1,0},{2,3},{3,2},{4,5},{5,4},{6,7},{7,6},{8,9},{9,8},{10,11... | collective-permute-start | bytes 1327112 | tf_op jit(solution)/shard_map/ppermute | solution.py:605
  758.1 22.5 %collective-permute-start.53 = (bf16[96,2304]{1,0:T(8,128)(2,1)S(1)}, bf16[96,2304]{1,0:T(8,128)(2,1)S(1)}, u32[]{:S(2)}, u32[]{:S(2)}) collective-permute-start(bf16[96,2304]{1,0:T(8,128)(2,1)S(1)} %get-tuple-element.94), channel_id=1, source_target_pairs={{0,2},{1,3},{2,0},{3,1},{4,6},{5,7},{6,4},{7,5},{8,10},{9,11},{10,... | collective-permute-start | bytes 1327112 | tf_op jit(solution)/shard_map/ppermute | solution.py:605
  758.7 22.0 %collective-permute-start.54 = (bf16[96,2304]{1,0:T(8,128)(2,1)S(1)}, bf16[96,2304]{1,0:T(8,128)(2,1)S(1)}, u32[]{:S(2)}, u32[]{:S(2)}) collective-permute-start(bf16[96,2304]{1,0:T(8,128)(2,1)S(1)} %get-tuple-element.93), channel_id=1, source_target_pairs={{0,3},{1,2},{2,1},{3,0},{4,7},{5,6},{6,5},{7,4},{8,11},{9,10},{10,... | collective-permute-start | bytes 1327112 | tf_op jit(solution)/shard_map/ppermute | solution.py:605
  761.7 26.4 %collective-permute-start.38 = (bf16[96,2304]{1,0:T(8,128)(2,1)S(1)}, bf16[96,2304]{1,0:T(8,128)(2,1)S(1)}, u32[]{:S(2)}, u32[]{:S(2)}) collective-permute-start(bf16[96,2304]{1,0:T(8,128)(2,1)S(1)} %get-tuple-element.95), channel_id=1, source_target_pairs={{0,1},{1,0},{2,3},{3,2},{4,5},{5,4},{6,7},{7,6},{8,9},{9,8},{10,11... | collective-permute-start | bytes 1327112 | tf_op jit(solution)/shard_map/ppermute | solution.py:605
  763.7 35.1 %collective-permute-start.39 = (bf16[96,2304]{1,0:T(8,128)(2,1)S(1)}, bf16[96,2304]{1,0:T(8,128)(2,1)S(1)}, u32[]{:S(2)}, u32[]{:S(2)}) collective-permute-start(bf16[96,2304]{1,0:T(8,128)(2,1)S(1)} %get-tuple-element.97), channel_id=1, source_target_pairs={{0,2},{1,3},{2,0},{3,1},{4,6},{5,7},{6,4},{7,5},{8,10},{9,11},{10,... | collective-permute-start | bytes 1327112 | tf_op jit(solution)/shard_map/ppermute | solution.py:605
  769.1 29.7 %collective-permute-start.40 = (bf16[96,2304]{1,0:T(8,128)(2,1)S(1)}, bf16[96,2304]{1,0:T(8,128)(2,1)S(1)}, u32[]{:S(2)}, u32[]{:S(2)}) collective-permute-start(bf16[96,2304]{1,0:T(8,128)(2,1)S(1)} %get-tuple-element.96), channel_id=1, source_target_pairs={{0,3},{1,2},{2,1},{3,0},{4,7},{5,6},{6,5},{7,4},{8,11},{9,10},{10,... | collective-permute-start | bytes 1327112 | tf_op jit(solution)/shard_map/ppermute | solution.py:605
  780.9 18.3 %collective-permute-start.55 = (bf16[96,2304]{1,0:T(8,128)(2,1)S(1)}, bf16[96,2304]{1,0:T(8,128)(2,1)S(1)}, u32[]{:S(2)}, u32[]{:S(2)}) collective-permute-start(bf16[96,2304]{1,0:T(8,128)(2,1)S(1)} %fusion.3), channel_id=1, source_target_pairs={{0,8},{4,12},{8,0},{12,4},{16,24},{20,28},{24,16},{28,20},{1,9},{5... | collective-permute-start | bytes 1327112 | tf_op jit(solution)/shard_map/ppermute | solution.py:605
  799.0 19.6 %collective-permute-start.41 = (bf16[96,2304]{1,0:T(8,128)(2,1)S(1)}, bf16[96,2304]{1,0:T(8,128)(2,1)S(1)}, u32[]{:S(2)}, u32[]{:S(2)}) collective-permute-start(bf16[96,2304]{1,0:T(8,128)(2,1)S(1)} %fusion.6), channel_id=1, source_target_pairs={{0,8},{4,12},{8,0},{12,4},{16,24},{20,28},{24,16},{28,20},{1,9},{5... | collective-permute-start | bytes 1327112 | tf_op jit(solution)/shard_map/ppermute | solution.py:605
  799.2 31.4 %collective-permute-start.56 = (bf16[96,2304]{1,0:T(8,128)(2,1)S(1)}, bf16[96,2304]{1,0:T(8,128)(2,1)S(1)}, u32[]{:S(2)}, u32[]{:S(2)}) collective-permute-start(bf16[96,2304]{1,0:T(8,128)(2,1)S(1)} %add_convert_fusion.5), channel_id=1, source_target_pairs={{0,16},{4,20},{8,24},{12,28},{16,0},{20,4},{24,8},{28,12},{1,17},{... | collective-permute-start | bytes 1327112 | tf_op jit(solution)/shard_map/ppermute | solution.py:605
  818.8 21.3 %collective-permute-start.42 = (bf16[96,2304]{1,0:T(8,128)(2,1)S(1)}, bf16[96,2304]{1,0:T(8,128)(2,1)S(1)}, u32[]{:S(2)}, u32[]{:S(2)}) collective-permute-start(bf16[96,2304]{1,0:T(8,128)(2,1)S(1)} %add_convert_fusion.7), channel_id=1, source_target_pairs={{0,16},{4,20},{8,24},{12,28},{16,0},{20,4},{24,8},{28,12},{1,17},{... | collective-permute-start | bytes 1327112 | tf_op jit(solution)/shard_map/ppermute | solution.py:605
  830.8 9.5 %collective-permute-start.57 = (bf16[96,2304]{1,0:T(8,128)(2,1)S(1)}, bf16[96,2304]{1,0:T(8,128)(2,1)S(1)}, u32[]{:S(2)}, u32[]{:S(2)}) collective-permute-start(bf16[96,2304]{1,0:T(8,128)(2,1)S(1)} %add_convert_fusion.4), channel_id=1, source_target_pairs={{0,4},{4,0},{8,12},{12,8},{16,20},{20,16},{24,28},{28,24},{1,5},{5... | collective-permute-start | bytes 1327112 | tf_op jit(solution)/shard_map/ppermute | solution.py:605
  840.2 1.9 collective-permute-start.43
  (25 other events, 360.3 us)
